TPU v7x, 32 devices: a whole 2x2x4 slice. The times are simulated.
32 devices in a mesh: group: 4 (over y, x), hidden: 8 (over z, core).
Axes of the slice: x: 2, y: 2, z: 4, core: 2. Of those that a mesh axis runs over, the one named last changes fastest.
Arguments:
- queries: bfloat16 [1536, 4096], P('group', 'hidden'), may hold values from -16 to 16, as said below
- key_rows: bfloat16 [1536, 512], P('group'), may hold values from -16 to 16
- value_rows: bfloat16 [1536, 512], P('group'), may hold values from -6 to 6
- out_proj: bfloat16 [4096, 2048], P('hidden'), may hold values from -0.09375 to 0.09375
- residual: bfloat16 [1536, 2048], P('group'), may hold values from -120 to 120
- norm_gain: float32 [2048], replicated, may hold values from 0.1 to 1.9
- w_gate: bfloat16 [32, 2048, 768], P('group', None, 'hidden'), may hold values from -0.125 to 0.125
- w_up: bfloat16 [32, 2048, 768], P('group', None, 'hidden'), may hold values from -0.125 to 0.125
- w_down: bfloat16 [32, 768, 2048], P('group', 'hidden'), may hold values from -0.21875 to 0.21875
- route_slot: int32 [1536, 8], P('group'), may hold values from 0 to 15, all different within a row; in each aligned block of 384 rows (0 to 383, 384 to 767, ...) at most 240 rows name the same one
- route_weight: float32 [1536, 8], P('group'), may hold values from 0.05 to 0.3
- fetch_list: int32 [4, 16], replicated, may hold values from 0 to 31, as said below
- cotangent: bfloat16 [1536, 2048], P('group'), may hold values from -6 to 6
Outputs:
- layer_out: bfloat16 [1536, 2048], P('group', 'hidden')
- grad_normed: bfloat16 [1536, 2048], P('group', 'hidden')
- grad_gate: bfloat16 [32, 2048, 768], P('group', None, 'hidden')
- grad_up: bfloat16 [32, 2048, 768], P('group', None, 'hidden')
- grad_down: bfloat16 [32, 768, 2048], P('group', 'hidden')
Inputs may be any that keep to these rules, and one draw needn't show every extreme that they name: `queries`: queries and keys lie within the range. `route_slot`: within each group's 384 tokens no entry is named by more than 240 tokens, a bound that some block reaches; a token's 8 entries differ. `fetch_list`: entry f of every group's list is an expert owned by owner group f // 4, that is an id from (f // 4) * 8 to (f // 4) * 8 + 7; the ids of one group's list differ.
All inputs are finite; a program needn't handle non-finite values.
Results may differ from a plain program's by a relative error of at most 0.017.
Values may be sent and summed in bfloat16 or wider, within the bound.
A program may use at most 256 MiB of HBM per device.

v0:
```python
import functools
import math

import jax
import jax.numpy as jnp
from jax import lax
from jax.experimental import pallas as pl
from jax.experimental.pallas import tpu as pltpu
from jax.sharding import PartitionSpec as P

HEADS = 32
KV_HEADS = 4
HEAD_DIM = 128
EXP_GROUP = 8
FETCH = 16

epsilon = 1e-06


def attention_rows(query_in, key_block, value_block, heads_here):
    tokens_here = query_in.shape[0]
    query_heads = query_in.reshape(tokens_here, heads_here, HEAD_DIM)
    pos = jnp.arange(tokens_here, dtype=jnp.int32)
    scores = jnp.einsum(
        "thd,sd->hts", query_heads, key_block, preferred_element_type=jnp.float32
    ) / math.sqrt(HEAD_DIM)
    scores = jnp.where(pos[:, None] >= pos[None, :], scores, -1e30)
    row_peak = jnp.max(scores, axis=-1, keepdims=True)
    weights = jnp.exp(scores - row_peak)
    probabilities = (weights / jnp.sum(weights, axis=-1, keepdims=True)).astype(jnp.bfloat16)
    mixed = jnp.einsum("hts,sd->thd", probabilities, value_block, preferred_element_type=jnp.float32)
    return mixed.astype(jnp.bfloat16).reshape(tokens_here, heads_here * HEAD_DIM)


def dot(a, b, dims=((1,), (0,))):
    return lax.dot_general(a, b, (dims, ((), ())), preferred_element_type=jnp.float32)


def expert_kernel(per_owner, ids_ref, *refs):
    gates, refs = refs[:per_owner], refs[per_owner:]
    ups, refs = refs[:per_owner], refs[per_owner:]
    downs, refs = refs[:per_owner], refs[per_owner:]
    (
        y_ref, scale_ref,
        part_ref, gate_out, up_out, down_out,
        x2d, c2d, w_in, w_out, act, grads, act_turned, grads_turned, acc_gate, acc_up, acc_down, sems,
    ) = refs
    step = pl.program_id(0)
    blocks, width = y_ref.shape[1], y_ref.shape[4]
    tokens = x2d.shape[0]
    units = gates[0].shape[1]
    half = per_owner * units

    @pl.when(step == 0)
    def _():
        acc_gate[...] = jnp.zeros_like(acc_gate)
        acc_up[...] = jnp.zeros_like(acc_up)
        acc_down[...] = jnp.zeros_like(acc_down)

    for s in range(per_owner):
        w_in[s * units : (s + 1) * units, :] = gates[s][0]
        w_in[half + s * units : half + (s + 1) * units, :] = ups[s][0]
        w_out[s * units : (s + 1) * units, :] = downs[s][0]
    for h in range(blocks):
        x2d[:, h * width : (h + 1) * width] = y_ref[0, h, 0, :tokens]
        c2d[:, h * width : (h + 1) * width] = y_ref[0, h, 1, :tokens]

    scale = scale_ref[0]
    inverse = scale[:, per_owner : per_owner + 1]
    lane = lax.broadcasted_iota(jnp.int32, (tokens, half), 1)
    weight = jnp.broadcast_to(scale[:, :1], (tokens, half))
    for s in range(1, per_owner):
        weight = jnp.where(lane >= s * units, scale[:, s : s + 1], weight)
    turned = ((1,), (1,))
    pre_gate = dot(x2d[...], w_in[:half, :], turned) * inverse
    pre_up = dot(x2d[...], w_in[half:, :], turned) * inverse
    d_act = dot(c2d[...], w_out[...], turned) * weight
    sig = jax.nn.sigmoid(pre_gate)
    swish = pre_gate * sig
    weighted = swish * pre_up * weight
    d_gate = d_act * pre_up * sig * (1.0 + pre_gate * (1.0 - sig))
    d_up = d_act * swish
    act[...] = weighted.astype(act.dtype)
    grads[:, :half] = d_gate.astype(grads.dtype)
    grads[:, half:] = d_up.astype(grads.dtype)
    act_turned[...] = act[...].T
    grads_turned[:half, :] = (d_gate * inverse).astype(grads.dtype).T
    grads_turned[half:, :] = (d_up * inverse).astype(grads.dtype).T

    step_ids = [ids_ref[step * per_owner + s] for s in range(per_owner)]

    def add(acc, e, cols, value):
        acc[e, :, cols] = (acc[e, :, cols].astype(jnp.float32) + value).astype(acc.dtype)

    @pl.loop(0, blocks)
    def _(h):
        cols = pl.ds(pl.multiple_of(h * width, width), width)
        part_ref[0, h, 0] = dot(act[...], w_out[:, cols]).astype(part_ref.dtype)
        part_ref[0, h, 1] = dot(grads[...], w_in[:, cols]).astype(part_ref.dtype)
        down = dot(act_turned[...], c2d[:, cols])
        both = dot(grads_turned[...], x2d[:, cols])
        for s in range(per_owner):
            rows = slice(s * units, (s + 1) * units)
            add(acc_down, step_ids[s], cols, down[rows])
            add(acc_gate, step_ids[s], cols, both[rows])
            add(acc_up, step_ids[s], cols, both[half:][rows])

    @pl.when(step == pl.num_programs(0) - 1)
    def _():
        copies = [
            pltpu.make_async_copy(a, b, sems.at[i])
            for i, (a, b) in enumerate(
                ((acc_gate, gate_out), (acc_up, up_out), (acc_down, down_out))
            )
        ]
        for copy in copies:
            copy.start()
        for copy in copies:
            copy.wait()


def gather_kernel(groups, hidden, y_ref, out_ref, local_sem, send_sems, recv_sems):
    g, h = lax.axis_index("group"), lax.axis_index("hidden")
    chips = hidden // 2
    rows_all = y_ref.shape[1]
    cut = rows_all // 32 * 16
    rows = (pl.ds(0, cut), pl.ds(cut, rows_all - cut))
    ahead = {"group": g, "hidden": lax.rem(h + 2, hidden)}
    behind = {"group": g, "hidden": lax.rem(h + hidden - 2, hidden)}
    partner = {"group": g, "hidden": h + 1 - 2 * lax.rem(h, 2)}
    peers = [{"group": lax.rem(g + k, groups), "hidden": h} for k in range(groups)]
    mesh_id = pl.DeviceIdType.MESH

    barrier = pltpu.get_barrier_semaphore()
    greeted = [ahead, behind, partner] + peers[1:]
    for device in greeted:
        pl.semaphore_signal(barrier, inc=1, device_id=device, device_id_type=mesh_id)
    pl.semaphore_wait(barrier, len(greeted))

    made = {}

    def send(key, source, g_from, h_from, part, device):
        number = len(made)
        target = out_ref.at[g_from, h_from, :, rows[part]]
        copy = pltpu.make_async_remote_copy(
            src_ref=target if source is None else source,
            dst_ref=target,
            send_sem=send_sems.at[number],
            recv_sem=recv_sems.at[number],
            device_id=device,
            device_id_type=mesh_id,
        )
        copy.start()
        made[key] = copy

    local = pltpu.make_async_copy(y_ref, out_ref.at[g, h], local_sem)
    local.start()
    own = [y_ref.at[:, rows[0]], y_ref.at[:, rows[1]]]
    group_of = [lax.rem(g + groups - k, groups) for k in range(groups)]
    hidden_of = [lax.rem(h + hidden - 2 * t, hidden) for t in range(chips)]
    send(("ring0", 1), own[0], g, h, 0, ahead)
    for k in range(1, groups):
        send(("peer1", 0, k), own[1], g, h, 1, peers[k])
    send(("ring1", 1, 0), own[1], g, h, 1, ahead)
    for k in range(1, groups):
        send(("peer0", 0, k), own[0], g, h, 0, peers[k])
    for part in range(2):
        send(("pair", part, 0, 0), own[part], g, h, part, partner)

    def arrive0(t):
        made[("ring0", t)].wait_recv()
        if t + 1 < chips:
            send(("ring0", t + 1), None, g, hidden_of[t], 0, ahead)
        for k in range(1, groups):
            send(("peer0", t, k), None, g, hidden_of[t], 0, peers[k])
        send(("pair", 0, t, 0), None, g, hidden_of[t], 0, partner)

    def arrive1(t, k):
        made[("ring1", t, k)].wait_recv()
        if t + 1 < chips:
            send(("ring1", t + 1, k), None, group_of[k], hidden_of[t], 1, ahead)
        send(("pair", 1, t, k), None, group_of[k], hidden_of[t], 1, partner)

    def arrive_peer(t, k):
        made[("peer0", t, k)].wait_recv()
        send(("pair", 0, t, k), None, group_of[k], hidden_of[t], 0, partner)

    arrive0(1)
    for k in range(1, groups):
        made[("peer1", 0, k)].wait_recv()
        send(("ring1", 1, k), None, group_of[k], h, 1, ahead)
        send(("pair", 1, 0, k), None, group_of[k], h, 1, partner)
    for t in range(1, chips):
        if t > 1:
            arrive0(t)
        for k in range(1, groups):
            arrive_peer(t - 1, k)
        for k in range(groups):
            arrive1(t, k)
    for k in range(1, groups):
        arrive_peer(chips - 1, k)
    for key, copy in made.items():
        if key[0] == "pair":
            copy.wait_recv()
        copy.wait_send()
    local.wait()


def gather_all(y, groups, hidden):
    chips = hidden // 2
    copies = (chips - 1) * (1 + groups) + (groups - 1) * (1 + chips) + 2 * chips * groups
    return pl.pallas_call(
        functools.partial(gather_kernel, groups, hidden),
        out_shape=jax.ShapeDtypeStruct((groups, hidden) + y.shape, y.dtype),
        in_specs=[pl.BlockSpec(memory_space=pltpu.VMEM)],
        out_specs=pl.BlockSpec(memory_space=pl.ANY),
        scratch_shapes=[
            pltpu.SemaphoreType.DMA,
            pltpu.SemaphoreType.DMA((copies,)),
            pltpu.SemaphoreType.DMA((copies,)),
        ],
        compiler_params=pltpu.CompilerParams(collective_id=0, has_side_effects=True),
        name="gather_all",
    )(y)


def reduce_kernel(
    groups, hidden, parts_ref, out_ref,
    own, pair_in, peer_in0, peer_in1, ring_in0, ring_in1, local_sems, send_sems, recv_sems,
):
    g, h = lax.axis_index("group"), lax.axis_index("hidden")
    chips = hidden // 2
    tokens = out_ref.shape[1]
    cut = tokens // 32 * 16
    rows = (pl.ds(0, cut), pl.ds(cut, tokens - cut))
    ahead = {"group": g, "hidden": lax.rem(h + 2, hidden)}
    behind = {"group": g, "hidden": lax.rem(h + hidden - 2, hidden)}
    partner_h = h + 1 - 2 * lax.rem(h, 2)
    partner = {"group": g, "hidden": partner_h}
    group_of = [lax.rem(g + k, groups) for k in range(groups)]
    peers = [{"group": group_of[k], "hidden": h} for k in range(groups)]
    mesh_id = pl.DeviceIdType.MESH

    barrier = pltpu.get_barrier_semaphore()
    greeted = [ahead, behind, partner] + peers[1:]
    for device in greeted:
        pl.semaphore_signal(barrier, inc=1, device_id=device, device_id_type=mesh_id)
    pl.semaphore_wait(barrier, len(greeted))

    made = {}

    def send(key, source, target, device):
        number = len(made)
        copy = pltpu.make_async_remote_copy(
            src_ref=source,
            dst_ref=target,
            send_sem=send_sems.at[number],
            recv_sem=recv_sems.at[number],
            device_id=device,
            device_id_type=mesh_id,
        )
        copy.start()
        made[key] = copy

    def add(into, *others):
        total = into[...].astype(jnp.float32)
        for other in others:
            total = total + other[...].astype(jnp.float32)
        into[...] = total.astype(into.dtype)

    turns = list(range(1, chips)) + [0]
    loads = {}
    for t in turns:
        for k in range(groups):
            theirs = lax.rem(partner_h + hidden - 2 * t, hidden)
            send(("pair", t, k), parts_ref.at[group_of[k], theirs], pair_in.at[k, t], partner)
            mine = lax.rem(h + hidden - 2 * t, hidden)
            loads[t, k] = pltpu.make_async_copy(
                parts_ref.at[group_of[k], mine], own.at[k, t], local_sems.at[k * chips + t]
            )
            loads[t, k].start()

    def half(k, t, part):
        return own.at[k, t, :, rows[part]]

    last = chips - 1
    for t in turns:
        before = t - 1 if t else last
        for k in range(groups):
            loads[t, k].wait()
            made["pair", t, k].wait_recv()
            add(own.at[k, t], pair_in.at[k, t])
            if t == 1:
                send(("ring1", t, k), half(k, t, 1), ring_in1.at[t, k], ahead)
            if k:
                send(("peer0", t, k), half(k, t, 0), peer_in0.at[t, k], peers[k])
        if t != 1:
            for k in list(range(1, groups)) + [0]:
                made["ring1", before, k].wait_recv()
                add(half(k, t, 1), ring_in1.at[before, k])
                if t:
                    send(("ring1", t, k), half(k, t, 1), ring_in1.at[t, k], ahead)
                elif k:
                    send(("peer1", 0, k), half(k, t, 1), peer_in1.at[k], peers[k])
        arrived = []
        for k in range(1, groups):
            made["peer0", t, k].wait_recv()
            arrived.append(peer_in0.at[t, k])
        if t != 1:
            made["ring0", before].wait_recv()
            arrived.append(ring_in0.at[before])
        add(half(0, t, 0), *arrived)
        if t:
            send(("ring0", t), half(0, t, 0), ring_in0.at[t], ahead)
    for k in range(1, groups):
        made["peer1", 0, k].wait_recv()
    add(half(0, 0, 1), *[peer_in1.at[k] for k in range(1, groups)])
    out_ref[...] = own[0, 0]
    for copy in made.values():
        copy.wait_send()


def reduce_parts(parts, collective_id):
    groups, hidden, pieces, tokens, width = parts.shape
    chips = hidden // 2
    block = 2 * pieces * tokens * width
    if 3 * groups * chips * block > 40 << 20:
        flat = parts.reshape((groups * hidden,) + parts.shape[2:])
        return lax.psum_scatter(flat, ("group", "hidden"), scatter_dimension=0, tiled=True)[0]
    copies = (chips - 1) * (1 + groups) + (groups - 1) * (1 + chips) + chips * groups
    cut = tokens // 32 * 16
    first, second = (pieces, cut, width), (pieces, tokens - cut, width)
    bf = parts.dtype
    return pl.pallas_call(
        functools.partial(reduce_kernel, groups, hidden),
        out_shape=jax.ShapeDtypeStruct(parts.shape[2:], bf),
        in_specs=[pl.BlockSpec(memory_space=pl.ANY)],
        out_specs=pl.BlockSpec(memory_space=pltpu.VMEM),
        scratch_shapes=[
            pltpu.VMEM((groups, chips) + parts.shape[2:], bf),
            pltpu.VMEM((groups, chips) + parts.shape[2:], bf),
            pltpu.VMEM((chips, groups) + first, bf),
            pltpu.VMEM((groups,) + second, bf),
            pltpu.VMEM((chips,) + first, bf),
            pltpu.VMEM((chips, groups) + second, bf),
            pltpu.SemaphoreType.DMA((chips * groups,)),
            pltpu.SemaphoreType.DMA((copies,)),
            pltpu.SemaphoreType.DMA((copies,)),
        ],
        compiler_params=pltpu.CompilerParams(
            collective_id=collective_id, has_side_effects=True, vmem_limit_bytes=40 << 20
        ),
        name=f"reduce_parts_{collective_id}",
    )(parts)


def to_rows(values, rows, width):
    high = lax.reduce_precision(values, 8, 7)
    rest = values - high
    mid = lax.reduce_precision(rest, 8, 7)
    flat = jnp.stack([high, mid, rest - mid]).reshape(-1).astype(jnp.bfloat16)
    return jnp.pad(flat, (0, rows * width - flat.shape[0])).reshape(rows, width)


def from_rows(block, count):
    flat = block.reshape(block.shape[:2] + (-1,))[:, :, : 3 * count].astype(jnp.float32)
    high, mid, low = (flat[:, :, i * count : (i + 1) * count] for i in range(3))
    return high + mid + low


def experts(order, ids, y, scale, w_gate, w_up, w_down):
    groups, blocks, _, rows, width = y.shape
    tokens = scale.shape[1]
    model = blocks * width
    per_owner = ids.shape[1]
    units = w_down.shape[1]
    half = per_owner * units
    ids_end = groups * per_owner

    def pick(s):
        return pl.BlockSpec((1, units, model), lambda k, n: (n[k * per_owner + s], 0, 0))

    bf = jnp.bfloat16
    parts = jax.ShapeDtypeStruct((groups, blocks, 2, tokens, width), bf)
    return pl.pallas_call(
        functools.partial(expert_kernel, per_owner),
        grid_spec=pltpu.PrefetchScalarGridSpec(
            num_scalar_prefetch=1,
            grid=(groups,),
            in_specs=[pick(s) for s in range(per_owner)] * 3
            + [
                pl.BlockSpec(
                    (1, blocks, 2, rows, width), lambda k, n: (n[ids_end + k], 0, 0, 0, 0)
                ),
                pl.BlockSpec(
                    (1, tokens, scale.shape[2]), lambda k, n: (n[ids_end + k], 0, 0)
                ),
            ],
            out_specs=[
                pl.BlockSpec((1,) + parts.shape[1:], lambda k, n: (n[ids_end + k], 0, 0, 0, 0)),
            ]
            + [pl.BlockSpec(memory_space=pl.ANY)] * 3,
            scratch_shapes=[
                pltpu.VMEM((tokens, model), bf),
                pltpu.VMEM((tokens, model), bf),
                pltpu.VMEM((2 * half, model), bf),
                pltpu.VMEM((half, model), bf),
                pltpu.VMEM((tokens, half), bf),
                pltpu.VMEM((tokens, 2 * half), bf),
                pltpu.VMEM((half, tokens), bf),
                pltpu.VMEM((2 * half, tokens), bf),
                pltpu.VMEM(w_down.shape, bf),
                pltpu.VMEM(w_down.shape, bf),
                pltpu.VMEM(w_down.shape, bf),
                pltpu.SemaphoreType.DMA((3,)),
            ],
        ),
        out_shape=[parts] + [jax.ShapeDtypeStruct(w_down.shape, bf)] * 3,
        compiler_params=pltpu.CompilerParams(vmem_limit_bytes=56 << 20),
        name="experts",
    )(
        jnp.concatenate([ids.reshape(-1), order]),
        *([w_gate] * per_owner + [w_up] * per_owner + [w_down] * per_owner),
        y,
        scale,
    )


def shards(
    queries,
    key_rows,
    value_rows,
    out_proj,
    residual,
    norm_gain,
    w_gate,
    w_up,
    w_down,
    route_slot,
    route_weight,
    fetch_list,
    cotangent,
):
    tokens_here, model = cotangent.shape
    hidden_index = lax.axis_index("hidden")
    hidden_count = lax.axis_size("hidden")
    group_index = lax.axis_index("group")
    group_count = lax.axis_size("group")
    per_owner = FETCH // group_count

    chosen = route_slot[:, :, None] == jnp.arange(FETCH, dtype=jnp.int32)[None, None, :]
    slot_weight = jnp.sum(jnp.where(chosen, route_weight[:, :, None], 0.0), axis=1)
    order = (group_index + jnp.arange(group_count, dtype=jnp.int32)) % group_count
    own_cols = lax.dynamic_slice_in_dim(fetch_list, group_index * per_owner, per_owner, 1)
    ids = jnp.take(own_cols - group_index * EXP_GROUP, order, axis=0)

    heads_here = queries.shape[1] // HEAD_DIM
    kv_index = hidden_index * heads_here // (HEADS // KV_HEADS)
    key_block = lax.dynamic_slice_in_dim(key_rows, kv_index * HEAD_DIM, HEAD_DIM, 1)
    value_block = lax.dynamic_slice_in_dim(value_rows, kv_index * HEAD_DIM, HEAD_DIM, 1)
    mixed = attention_rows(queries, key_block, value_block, heads_here)
    partial_value = jnp.dot(mixed, out_proj, preferred_element_type=jnp.float32)
    share_width = model // hidden_count
    first_col = hidden_index * share_width
    blocks = partial_value.astype(jnp.bfloat16).reshape(tokens_here, hidden_count, share_width)
    attn_share = reduce_parts(jnp.swapaxes(blocks, 0, 1)[None, :, None], 2)[0]
    stream = lax.dynamic_slice_in_dim(residual, first_col, share_width, 1).astype(
        jnp.float32
    ) + attn_share.astype(jnp.float32)
    gain = lax.dynamic_slice_in_dim(norm_gain, first_col, share_width, 0)
    squares = jnp.sum(stream * stream, axis=-1)
    gained = (stream * gain).astype(jnp.bfloat16)
    slots_here = FETCH // hidden_count
    slots = lax.dynamic_slice_in_dim(slot_weight.T, hidden_index * slots_here, slots_here, 0)
    extra = -(-3 * slots_here * tokens_here // (16 * share_width)) * 16
    cot_share = lax.dynamic_slice_in_dim(cotangent, first_col, share_width, 1)
    y = jnp.stack(
        [
            jnp.concatenate([gained, to_rows(squares, extra, share_width)]),
            jnp.concatenate([cot_share, to_rows(slots, extra, share_width)]),
        ]
    )
    y_all = gather_all(y, group_count, hidden_count)
    squares_all = from_rows(y_all[:, :, 0, tokens_here:], tokens_here).sum(axis=1)
    inverse = lax.rsqrt(squares_all / model + epsilon)
    weights = from_rows(y_all[:, :, 1, tokens_here:], slots_here * tokens_here)
    weights = weights.reshape(group_count, FETCH, tokens_here)
    weights = lax.dynamic_slice_in_dim(weights, group_index * per_owner, per_owner, 1)
    scale = jnp.concatenate([weights, inverse[:, None, :]], axis=1)
    scale = jnp.pad(scale, ((0, 0), (0, 8 - scale.shape[1]), (0, 0)))
    scale = jnp.swapaxes(scale, 1, 2)
    parts, grad_gate, grad_up, grad_down = experts(
        order,
        ids,
        y_all,
        scale,
        jnp.swapaxes(w_gate, 1, 2),
        jnp.swapaxes(w_up, 1, 2),
        w_down,
    )
    grad_gate = jnp.swapaxes(grad_gate, 1, 2)
    grad_up = jnp.swapaxes(grad_up, 1, 2)
    sums = reduce_parts(parts, 1)
    layer_out = (stream + sums[0].astype(jnp.float32)).astype(jnp.bfloat16)
    return (layer_out, sums[1], grad_gate, grad_up, grad_down)


def solution(mesh):
    return jax.shard_map(
        shards,
        mesh=mesh,
        in_specs=(
            P("group", "hidden"),
            P("group", None),
            P("group", None),
            P("hidden", None),
            P("group", None),
            P(),
            P("group", None, "hidden"),
            P("group", None, "hidden"),
            P("group", "hidden", None),
            P("group", None),
            P("group", None),
            P(),
            P("group", None),
        ),
        out_specs=(
            P("group", "hidden"),
            P("group", "hidden"),
            P("group", None, "hidden"),
            P("group", None, "hidden"),
            P("group", "hidden", None),
        ),
        check_vma=False,
    )
```

profile of v0, /device:TPU:0, one launch (start us, length us, event | category | flops | bytes accessed | tf_op | source)
XLA Modules:
  0.0 251.5 jit_solution(937364693513730816)
XLA Ops:
  0.6 0.0 copy-start
  0.7 0.9 dynamic_slice.28
  1.6 0.8 dynamic-slice_subtract_fusion
  2.4 0.6 gather_fusion
  2.9 0.1 broadcast_select_fusion
  3.0 0.1 select_n.80
  3.1 0.6 pad_add_fusion.ids_ref
  3.7 0.8 select_reduce_fusion
  4.6 0.9 constant_dynamic-slice_fusion.1
  5.5 3.4 %fusion.42 = (f32[4,384]{1,0:T(4,128)S(1)}, f32[4,384,384]{1,2,0:T(8,128)}) fusion(pred[384,384]{0,1:T(8,128)(4,1)S(1)} %iota_compare_fusion.1, bf16[384,512]{1,0:T(8,128)(2,1)} %param.14, s32[]{:T(128)S(6)} %select_n.72, bf16[384,512]{1,0:T(8,128)(2,1)} %param.13), kind=kOutput, calls=%fused_computation.82 | convolution fusion | flops 153354624 | bytes 3004420 | tf_op jit(solution)/shard_map/sub | solution.py:29
  8.9 2.1 convolution_convert_fusion.1
  11.1 0.0 copy-done
  11.1 2.2 convolution_convert_fusion
  13.2 2.6 %copy.44 = bf16[384,2048]{0,1:T(8,128)(2,1)} copy(bf16[384,2048]{1,0:T(8,128)(2,1)} %convolution_convert_fusion) | data formatting | bytes 3145728 | tf_op jit(solution)/shard_map/convert_element_type | solution.py:465
  15.8 2.6 %copy.45 = bf16[384,8,256]{2,0,1:T(8,128)(2,1)} copy(bf16[384,8,256]{0,2,1:T(8,128)(2,1)} %bitcast.98) | data formatting | bytes 3145728 | tf_op jit(solution)/shard_map/reshape | solution.py:465
  18.4 1.4 copy-done.2
  19.8 21.0 %reduce_parts_2.1 = bf16[1,384,256]{2,1,0:T(8,128)(2,1)S(1)} custom-call(bf16[1,8,1,384,256]{4,3,2,1,0:T(8,128)(2,1)S(1)} %bitcast.89), custom_call_target="tpu_custom_call" | custom-call | tf_op jit(solution)/shard_map/reduce_parts_2/pallas_call | solution.py:334
  40.8 1.1 multiply_convert_fusion
  42.0 0.8 pad_maximum_fusion.y_ref
  42.8 75.4 %gather_all.1.refs_12_ = bf16[4,8,2,400,256]{4,3,2,1,0:T(8,128)(2,1)} custom-call(bf16[2,400,256]{2,1,0:T(8,128)(2,1)} %pad_maximum_fusion.y_ref), custom_call_target="tpu_custom_call" | custom-call | tf_op jit(solution)/shard_map/gather_all/pallas_call | solution.py:212
  118.1 1.1 fusion.41
  119.2 0.1 reshape_squeeze.6
  119.5 0.1 reshape_squeeze.7
  119.7 0.3 copy.50
  120.0 1.2 copy.47
  121.2 2.4 fusion.5.refs_13_
  123.5 48.5 %experts.1 = (bf16[4,8,2,384,256]{4,3,2,1,0:T(8,128)(2,1)}, bf16[8,96,2048]{2,1,0:T(8,128)(2,1)}, bf16[8,96,2048]{2,1,0:T(8,128)(2,1)}, bf16[8,96,2048]{2,1,0:T(8,128)(2,1)}) custom-call(s32[20]{0:T(128)} %pad_add_fusion.ids_ref, bf16[8,96,2048]{2,1,0:T(8,128)(2,1)} %bitcast.90, bf16[8,96,2048]{2,1,0:T(8,128)(2,1)} %bitcast.91, ...), custom_call_target="tpu_custom_call" | custom-call | tf_op jit(solution)/shard_map/experts/pallas_call | solution.py:385
  172.0 0.0 copy-start.1
  172.0 4.6 %copy-done.1 = bf16[4,8,2,384,256]{4,3,2,1,0:T(8,128)(2,1)S(1)} copy-done((bf16[4,8,2,384,256]{4,3,2,1,0:T(8,128)(2,1)S(1)}, bf16[4,8,2,384,256]{4,3,2,1,0:T(8,128)(2,1)}, u32[]{:S(2)}) %copy-start.1) | copy-done | bytes 12582936
  176.6 72.5 %reduce_parts_1.1 = bf16[2,384,256]{2,1,0:T(8,128)(2,1)S(1)} custom-call(bf16[4,8,2,384,256]{4,3,2,1,0:T(8,128)(2,1)S(1)} %copy-done.1), custom_call_target="tpu_custom_call" | custom-call | tf_op jit(solution)/shard_map/reduce_parts_1/pallas_call | solution.py:334
  249.1 1.7 fusion.9
  250.8 0.7 slice_bitcast_fusion
  (24 shorter events, 0.4 us)
Async XLA Ops:
  0.6 10.4 %copy-start = (bf16[512,2048]{1,0:T(8,128)(2,1)S(1)}, bf16[512,2048]{1,0:T(8,128)(2,1)}, u32[]{:S(2)}) copy-start(bf16[512,2048]{1,0:T(8,128)(2,1)} %param.16) | copy-start | bytes 6291460
  18.4 1.4 copy-start.2
  172.0 4.6 %copy-start.1 = (bf16[4,8,2,384,256]{4,3,2,1,0:T(8,128)(2,1)S(1)}, bf16[4,8,2,384,256]{4,3,2,1,0:T(8,128)(2,1)}, u32[]{:S(2)}) copy-start(bf16[4,8,2,384,256]{4,3,2,1,0:T(8,128)(2,1)} %get-tuple-element.9.parts_ref) | copy-start | bytes 37748740
where the time goes:
time: 252 us; the launch traced here: 251 us
  Pallas kernels  217 us (86%)
  local copies, waits for them, and re-layouts  17.2 us (7%)
  other arithmetic  8.37 us (3%)
  matrix products  7.67 us (3%)
    pallas_call x2, Pallas kernels, reduce_parts(): pl.pallas_call(functools.partial(reduce_kernel, groups, hidden), out_shap...  93.5 us
    pallas_call x1, Pallas kernels, gather_all(): pl.pallas_call(functools.partial(gather_kernel, groups, hidden), out_shap...  75.4 us
    pallas_call x1, Pallas kernels, experts(): pl.pallas_call(functools.partial(expert_kernel, per_owner), grid_spec=plt...  48.5 us
    unnamed x7, local copies, waits for them, and re-layouts  6.28 us

commit v1 on v0

--- a/solution.py
+++ b/solution.py
@@ -119,11 +119,15 @@
             copy.wait()
 
 
+def first_rows(count):
+    return count // 24 * 16
+
+
 def gather_kernel(groups, hidden, y_ref, out_ref, local_sem, send_sems, recv_sems):
     g, h = lax.axis_index("group"), lax.axis_index("hidden")
     chips = hidden // 2
     rows_all = y_ref.shape[1]
-    cut = rows_all // 32 * 16
+    cut = first_rows(rows_all)
     rows = (pl.ds(0, cut), pl.ds(cut, rows_all - cut))
     ahead = {"group": g, "hidden": lax.rem(h + 2, hidden)}
     behind = {"group": g, "hidden": lax.rem(h + hidden - 2, hidden)}
@@ -231,7 +235,7 @@
     g, h = lax.axis_index("group"), lax.axis_index("hidden")
     chips = hidden // 2
     tokens = out_ref.shape[1]
-    cut = tokens // 32 * 16
+    cut = first_rows(tokens)
     rows = (pl.ds(0, cut), pl.ds(cut, tokens - cut))
     ahead = {"group": g, "hidden": lax.rem(h + 2, hidden)}
     behind = {"group": g, "hidden": lax.rem(h + hidden - 2, hidden)}
@@ -328,7 +332,7 @@
         flat = parts.reshape((groups * hidden,) + parts.shape[2:])
         return lax.psum_scatter(flat, ("group", "hidden"), scatter_dimension=0, tiled=True)[0]
     copies = (chips - 1) * (1 + groups) + (groups - 1) * (1 + chips) + chips * groups
-    cut = tokens // 32 * 16
+    cut = first_rows(tokens)
     first, second = (pieces, cut, width), (pieces, tokens - cut, width)
     bf = parts.dtype
     return pl.pallas_call(

time: 252 us -> 234 us (0.929)
  Pallas kernels: 217 us -> 199 us
    pallas_call x1, Pallas kernels: 75.4 us -> 63.2 us  [gather_all(): pl.pallas_call(functools.partial(gather_kernel, groups, hidden), out_shap...]
    pallas_call x2, Pallas kernels: 93.5 us -> 87.2 us  [reduce_parts(): pl.pallas_call(functools.partial(reduce_kernel, groups, hidden), out_shap...]
where the time goes in v1:
time: 234 us; the launch traced here: 233 us
  Pallas kernels  199 us (85%)
  local copies, waits for them, and re-layouts  17.2 us (7%)
  other arithmetic  8.37 us (4%)
  matrix products  7.67 us (3%)
    pallas_call x2, Pallas kernels, reduce_parts(): pl.pallas_call(functools.partial(reduce_kernel, groups, hidden), out_shap...  87.2 us
    pallas_call x1, Pallas kernels, gather_all(): pl.pallas_call(functools.partial(gather_kernel, groups, hidden), out_shap...  63.2 us
    pallas_call x1, Pallas kernels, experts(): pl.pallas_call(functools.partial(expert_kernel, per_owner), grid_spec=plt...  48.7 us
    unnamed x7, local copies, waits for them, and re-layouts  6.28 us

profile of v1, /device:TPU:0, one launch (start us, length us, event | category | flops | bytes accessed | tf_op | source)
XLA Modules:
  0.0 233.2 jit_solution(15611340311509406741)
XLA Ops:
  0.6 0.0 copy-start
  0.7 0.9 dynamic_slice.28
  1.6 0.8 dynamic-slice_subtract_fusion
  2.4 0.6 gather_fusion
  2.9 0.1 broadcast_select_fusion
  3.0 0.1 select_n.80
  3.1 0.6 pad_add_fusion.ids_ref
  3.7 0.8 select_reduce_fusion
  4.6 0.9 constant_dynamic-slice_fusion.1
  5.5 3.4 %fusion.42 = (f32[4,384]{1,0:T(4,128)S(1)}, f32[4,384,384]{1,2,0:T(8,128)}) fusion(pred[384,384]{0,1:T(8,128)(4,1)S(1)} %iota_compare_fusion.1, bf16[384,512]{1,0:T(8,128)(2,1)} %param.14, s32[]{:T(128)S(6)} %select_n.72, bf16[384,512]{1,0:T(8,128)(2,1)} %param.13), kind=kOutput, calls=%fused_computation.82 | convolution fusion | flops 153354624 | bytes 3004420 | tf_op jit(solution)/shard_map/sub | solution.py:29
  8.9 2.1 convolution_convert_fusion.1
  11.1 0.0 copy-done
  11.1 2.2 convolution_convert_fusion
  13.2 2.6 %copy.44 = bf16[384,2048]{0,1:T(8,128)(2,1)} copy(bf16[384,2048]{1,0:T(8,128)(2,1)} %convolution_convert_fusion) | data formatting | bytes 3145728 | tf_op jit(solution)/shard_map/convert_element_type | solution.py:469
  15.8 2.6 %copy.45 = bf16[384,8,256]{2,0,1:T(8,128)(2,1)} copy(bf16[384,8,256]{0,2,1:T(8,128)(2,1)} %bitcast.98) | data formatting | bytes 3145728 | tf_op jit(solution)/shard_map/reshape | solution.py:469
  18.4 1.4 copy-done.2
  19.8 21.7 %reduce_parts_2.1 = bf16[1,384,256]{2,1,0:T(8,128)(2,1)S(1)} custom-call(bf16[1,8,1,384,256]{4,3,2,1,0:T(8,128)(2,1)S(1)} %bitcast.89), custom_call_target="tpu_custom_call" | custom-call | tf_op jit(solution)/shard_map/reduce_parts_2/pallas_call | solution.py:338
  41.5 1.1 multiply_convert_fusion
  42.7 0.8 pad_maximum_fusion.y_ref
  43.5 63.2 %gather_all.1.refs_12_ = bf16[4,8,2,400,256]{4,3,2,1,0:T(8,128)(2,1)} custom-call(bf16[2,400,256]{2,1,0:T(8,128)(2,1)} %pad_maximum_fusion.y_ref), custom_call_target="tpu_custom_call" | custom-call | tf_op jit(solution)/shard_map/gather_all/pallas_call | solution.py:216
  106.7 1.1 fusion.41
  107.8 0.1 reshape_squeeze.6
  108.0 0.1 reshape_squeeze.7
  108.2 0.3 copy.50
  108.5 1.2 copy.47
  109.7 2.4 %fusion.5.refs_13_ = f32[4,384,8]{2,1,0:T(8,128)} fusion(f32[4,1,384]{1,2,0:T(8,128)} %copy.47, f32[4,4,384]{1,2,0:T(8,128)S(1)} %copy.50), kind=kLoop, calls=%fused_computation.12 | loop fusion | flops 49152 | bytes 79872 | tf_op jit(solution)/shard_map/transpose | solution.py:495
  112.1 48.7 %experts.1 = (bf16[4,8,2,384,256]{4,3,2,1,0:T(8,128)(2,1)}, bf16[8,96,2048]{2,1,0:T(8,128)(2,1)}, bf16[8,96,2048]{2,1,0:T(8,128)(2,1)}, bf16[8,96,2048]{2,1,0:T(8,128)(2,1)}) custom-call(s32[20]{0:T(128)} %pad_add_fusion.ids_ref, bf16[8,96,2048]{2,1,0:T(8,128)(2,1)} %bitcast.90, bf16[8,96,2048]{2,1,0:T(8,128)(2,1)} %bitcast.91, ...), custom_call_target="tpu_custom_call" | custom-call | tf_op jit(solution)/shard_map/experts/pallas_call | solution.py:389
  160.8 0.0 copy-start.1
  160.8 4.6 %copy-done.1 = bf16[4,8,2,384,256]{4,3,2,1,0:T(8,128)(2,1)S(1)} copy-done((bf16[4,8,2,384,256]{4,3,2,1,0:T(8,128)(2,1)S(1)}, bf16[4,8,2,384,256]{4,3,2,1,0:T(8,128)(2,1)}, u32[]{:S(2)}) %copy-start.1) | copy-done | bytes 12582936
  165.4 65.4 %reduce_parts_1.1 = bf16[2,384,256]{2,1,0:T(8,128)(2,1)S(1)} custom-call(bf16[4,8,2,384,256]{4,3,2,1,0:T(8,128)(2,1)S(1)} %copy-done.1), custom_call_target="tpu_custom_call" | custom-call | tf_op jit(solution)/shard_map/reduce_parts_1/pallas_call | solution.py:338
  230.8 1.7 fusion.9
  232.5 0.7 slice_bitcast_fusion
  (24 shorter events, 0.4 us)
Async XLA Ops:
  0.6 10.4 %copy-start = (bf16[512,2048]{1,0:T(8,128)(2,1)S(1)}, bf16[512,2048]{1,0:T(8,128)(2,1)}, u32[]{:S(2)}) copy-start(bf16[512,2048]{1,0:T(8,128)(2,1)} %param.16) | copy-start | bytes 6291460
  18.4 1.4 copy-start.2
  160.8 4.6 %copy-start.1 = (bf16[4,8,2,384,256]{4,3,2,1,0:T(8,128)(2,1)S(1)}, bf16[4,8,2,384,256]{4,3,2,1,0:T(8,128)(2,1)}, u32[]{:S(2)}) copy-start(bf16[4,8,2,384,256]{4,3,2,1,0:T(8,128)(2,1)} %get-tuple-element.9.parts_ref) | copy-start | bytes 37748740

commit v2 on v1

--- a/solution.py
+++ b/solution.py
@@ -430,6 +430,315 @@
     )
 
 
+def pair_groups(g, i):
+    across, along = 1 - i // 2, 1 - lax.rem(i, 2)
+    gx, gy = lax.rem(g, 2), g // 2
+    return lax.rem(gy + along, 2) * 2 + lax.rem(gx + across, 2)
+
+
+def fused_kernel(
+    groups, hidden, per_owner,
+    ids_ref, seat_ref, y_ref, scale_ref, gate_ref, up_ref, down_ref,
+    out_ref, gate_out, up_out, down_out,
+    w_gate, w_up, w_down, xs, cs, w_in, w_out, act, grads, act_turned, grads_turned,
+    slot_gate, slot_up, slot_down, acc_gate, acc_up, acc_down,
+    own, stage, pair_in, peer_in0, peer_in1, ring_in0, ring_in1,
+    load_sems, fetch_sems, pair_sems, ring1_sems, peer0_sems, peer1_sems, ring0_sems,
+):
+    g, h = lax.axis_index("group"), lax.axis_index("hidden")
+    chips = hidden // 2
+    owned, units, model = w_gate.shape
+    tokens, width = out_ref.shape[1], out_ref.shape[2]
+    half = per_owner * units
+    last, final = chips - 1, groups - 1
+    cut = first_rows(tokens)
+    rows = (pl.ds(0, cut), pl.ds(cut, tokens - cut))
+    ahead = {"group": g, "hidden": lax.rem(h + 2, hidden)}
+    behind = {"group": g, "hidden": lax.rem(h + hidden - 2, hidden)}
+    partner_h = h + 1 - 2 * lax.rem(h, 2)
+    partner = {"group": g, "hidden": partner_h}
+    mesh_id = pl.DeviceIdType.MESH
+
+    def peer(i):
+        return {"group": pair_groups(g, i), "hidden": h}
+
+    barrier = pltpu.get_barrier_semaphore()
+    greeted = [ahead, behind, partner] + [peer(i) for i in range(final)]
+    for device in greeted:
+        pl.semaphore_signal(barrier, inc=1, device_id=device, device_id_type=mesh_id)
+
+    loads = [
+        pltpu.make_async_copy(a, b, load_sems.at[n])
+        for n, (a, b) in enumerate(((gate_ref, w_gate), (up_ref, w_up), (down_ref, w_down)))
+    ]
+    stores = [
+        pltpu.make_async_copy(a, b, load_sems.at[n])
+        for n, (a, b) in enumerate(((acc_gate, gate_out), (acc_up, up_out), (acc_down, down_out)))
+    ]
+
+    def fetches(i):
+        slot = lax.rem(i, 2)
+        source = pair_groups(g, i)
+        copies = []
+        for b in range(hidden):
+            for p, target in enumerate((xs, cs)):
+                copies.append(
+                    pltpu.make_async_copy(
+                        y_ref.at[source, b, p, pl.ds(0, tokens)],
+                        target.at[slot, :, pl.ds(b * width, width)],
+                        fetch_sems.at[slot, p, b],
+                    )
+                )
+        return copies
+
+    for copy in fetches(0):
+        copy.start()
+    for copy in loads:
+        copy.start()
+
+    acc_gate[...] = jnp.zeros_like(acc_gate)
+    acc_up[...] = jnp.zeros_like(acc_up)
+    acc_down[...] = jnp.zeros_like(acc_down)
+    for buffer in (slot_gate, slot_up, slot_down):
+        buffer[per_owner] = jnp.zeros(buffer.shape[1:], buffer.dtype)
+
+    def remote(source, target, sems, index, device):
+        return pltpu.make_async_remote_copy(
+            src_ref=source,
+            dst_ref=target,
+            send_sem=sems.at[(0,) + index],
+            recv_sem=sems.at[(1,) + index],
+            device_id=device,
+            device_id_type=mesh_id,
+        )
+
+    def part_of(i, t, part):
+        return own.at[i, t, :, rows[part]]
+
+    def pair_copy(i, t):
+        return remote(stage.at[i, t], pair_in.at[i, t], pair_sems, (i, t), partner)
+
+    def ring1_copy(i, t):
+        return remote(part_of(i, t, 1), ring_in1.at[i, t], ring1_sems, (i, t), ahead)
+
+    def peer0_copy(i, t):
+        return remote(part_of(i, t, 0), peer_in0.at[i, t], peer0_sems, (i, t), peer(i))
+
+    def peer1_copy(i):
+        return remote(part_of(i, 0, 1), peer_in1.at[i], peer1_sems, (i,), peer(i))
+
+    def ring0_copy(t):
+        return remote(part_of(final, t, 0), ring_in0.at[t], ring0_sems, (t,), ahead)
+
+    def add(into, *others):
+        total = into[...].astype(jnp.float32)
+        for other in others:
+            total = total + other[...].astype(jnp.float32)
+        into[...] = total.astype(into.dtype)
+
+    def pair_task(i, t):
+        pair_copy(i, t).wait_recv()
+        add(own.at[i, t], pair_in.at[i, t])
+
+        @pl.when(t == 1)
+        def _():
+            ring1_copy(i, t).start()
+
+        @pl.when(i < final)
+        def _():
+            peer0_copy(i, t).start()
+
+    def ring_task(i, t):
+        before = t - 1 if t else last
+        ring1_copy(i, before).wait_recv()
+        add(part_of(i, t, 1), ring_in1.at[i, before])
+        if t:
+            ring1_copy(i, t).start()
+
+    def finish_task(t):
+        arrived = []
+        for i in range(final):
+            peer0_copy(i, t).wait_recv()
+            arrived.append(peer_in0.at[i, t])
+        if t != 1:
+            before = t - 1 if t else last
+            ring0_copy(before).wait_recv()
+            arrived.append(ring_in0.at[before])
+        add(part_of(final, t, 0), *arrived)
+        if t:
+            ring0_copy(t).start()
+
+    pl.semaphore_wait(barrier, len(greeted))
+    for copy in loads:
+        copy.wait()
+
+    turned = ((1,), (1,))
+
+    @pl.loop(0, groups)
+    def _(i):
+        slot = lax.rem(i, 2)
+        group = pair_groups(g, i)
+
+        @pl.when(i < final)
+        def _():
+            for copy in fetches(i + 1):
+                copy.start()
+
+        for s in range(per_owner):
+            e = ids_ref[group * per_owner + s]
+            w_in[s * units : (s + 1) * units, :] = w_gate[e]
+            w_in[half + s * units : half + (s + 1) * units, :] = w_up[e]
+            w_out[s * units : (s + 1) * units, :] = w_down[e]
+        scale = scale_ref[group]
+        inverse = scale[:, per_owner : per_owner + 1]
+        lane = lax.broadcasted_iota(jnp.int32, (tokens, half), 1)
+        weight = jnp.broadcast_to(scale[:, :1], (tokens, half))
+        for s in range(1, per_owner):
+            weight = jnp.where(lane >= s * units, scale[:, s : s + 1], weight)
+        for copy in fetches(i):
+            copy.wait()
+        pre_gate = dot(xs[slot], w_in[:half, :], turned) * inverse
+        pre_up = dot(xs[slot], w_in[half:, :], turned) * inverse
+        d_act = dot(cs[slot], w_out[...], turned) * weight
+        sig = jax.nn.sigmoid(pre_gate)
+        swish = pre_gate * sig
+        weighted = swish * pre_up * weight
+        d_gate = d_act * pre_up * sig * (1.0 + pre_gate * (1.0 - sig))
+        d_up = d_act * swish
+        act[...] = weighted.astype(act.dtype)
+        grads[:, :half] = d_gate.astype(grads.dtype)
+        grads[:, half:] = d_up.astype(grads.dtype)
+        act_turned[...] = act[...].T
+        grads_turned[:half, :] = (d_gate * inverse).astype(grads.dtype).T
+        grads_turned[half:, :] = (d_up * inverse).astype(grads.dtype).T
+
+        @pl.loop(0, chips)
+        def _(j):
+            t = lax.rem(j + 1, chips)
+            back = hidden - 2 * t
+            for whose, target in ((partner_h, stage), (h, own)):
+                first = pl.multiple_of(lax.rem(whose + back, hidden) * width, width)
+                cols = pl.ds(first, width)
+                target[i, t, 0] = dot(act[...], w_out[:, cols]).astype(target.dtype)
+                target[i, t, 1] = dot(grads[...], w_in[:, cols]).astype(target.dtype)
+                if whose is partner_h:
+                    pair_copy(i, t).start()
+
+            @pl.when(j > 0)
+            def _():
+                pair_task(i, j)
+
+            @pl.when((i > 0) & (j == 1))
+            def _():
+                ring_task(i - 1, 0)
+                peer1_copy(i - 1).start()
+
+        pair_task(i, 0)
+        ring_task(i, 2)
+
+        @pl.when(i == final)
+        def _():
+            finish_task(1)
+
+        @pl.loop(0, hidden)
+        def _(b):
+            cols = pl.ds(pl.multiple_of(b * width, width), width)
+            down = dot(act_turned[...], cs[slot, :, cols])
+            both = dot(grads_turned[...], xs[slot, :, cols])
+            for s in range(per_owner):
+                slot_down[s] = down[s * units : (s + 1) * units]
+                slot_gate[s] = both[s * units : (s + 1) * units]
+                slot_up[s] = both[half + s * units : half + (s + 1) * units]
+            for e in range(owned):
+                seat = seat_ref[group * owned + e]
+                for total, value in ((acc_down, slot_down), (acc_gate, slot_gate), (acc_up, slot_up)):
+                    total[e, :, cols] = (total[e, :, cols].astype(jnp.float32) + value[seat]).astype(
+                        total.dtype
+                    )
+
+        ring_task(i, 3)
+
+    for copy in stores:
+        copy.start()
+    finish_task(2)
+    ring_task(final, 0)
+    finish_task(3)
+    finish_task(0)
+    for i in range(final):
+        peer1_copy(i).wait_recv()
+    add(part_of(final, 0, 1), *[peer_in1.at[i] for i in range(final)])
+    out_ref[...] = own[final, 0]
+    for i in range(groups):
+        for t in range(chips):
+            pair_copy(i, t).wait_send()
+            if t:
+                ring1_copy(i, t).wait_send()
+            if i < final:
+                peer0_copy(i, t).wait_send()
+    for i in range(final):
+        peer1_copy(i).wait_send()
+    for t in range(1, chips):
+        ring0_copy(t).wait_send()
+    for copy in stores:
+        copy.wait()
+
+
+def fused_experts(ids, seats, y, scale, w_gate, w_up, w_down, hidden):
+    groups = y.shape[0]
+    width = y.shape[4]
+    tokens = scale.shape[1]
+    chips = hidden // 2
+    owned, units, model = w_down.shape
+    per_owner = ids.shape[0] // groups
+    half = per_owner * units
+    cut = first_rows(tokens)
+    first, second = (2, cut, width), (2, tokens - cut, width)
+    block = (2, tokens, width)
+    bf = jnp.bfloat16
+    anywhere = pl.BlockSpec(memory_space=pl.ANY)
+    scalars = pl.BlockSpec(memory_space=pltpu.SMEM)
+    dma = pltpu.SemaphoreType.DMA
+    return pl.pallas_call(
+        functools.partial(fused_kernel, groups, hidden, per_owner),
+        in_specs=[scalars, scalars, anywhere, pl.BlockSpec(memory_space=pltpu.VMEM)] + [anywhere] * 3,
+        out_specs=[pl.BlockSpec(memory_space=pltpu.VMEM)] + [anywhere] * 3,
+        out_shape=[jax.ShapeDtypeStruct(block, bf)] + [jax.ShapeDtypeStruct(w_down.shape, bf)] * 3,
+        scratch_shapes=[pltpu.VMEM(w_down.shape, bf)] * 3
+        + [
+            pltpu.VMEM((2, tokens, model), bf),
+            pltpu.VMEM((2, tokens, model), bf),
+            pltpu.VMEM((2 * half, model), bf),
+            pltpu.VMEM((half, model), bf),
+            pltpu.VMEM((tokens, half), bf),
+            pltpu.VMEM((tokens, 2 * half), bf),
+            pltpu.VMEM((half, tokens), bf),
+            pltpu.VMEM((2 * half, tokens), bf),
+        ]
+        + [pltpu.VMEM((per_owner + 1, units, width), jnp.float32)] * 3
+        + [pltpu.VMEM(w_down.shape, bf)] * 3
+        + [
+            pltpu.VMEM((groups, chips) + block, bf),
+            pltpu.VMEM((groups, chips) + block, bf),
+            pltpu.VMEM((groups, chips) + block, bf),
+            pltpu.VMEM((groups - 1, chips) + first, bf),
+            pltpu.VMEM((groups - 1,) + second, bf),
+            pltpu.VMEM((chips,) + first, bf),
+            pltpu.VMEM((groups, chips) + second, bf),
+            dma((3,)),
+            dma((2, 2, hidden)),
+            dma((2, groups, chips)),
+            dma((2, groups, chips)),
+            dma((2, groups - 1, chips)),
+            dma((2, groups - 1)),
+            dma((2, chips)),
+        ],
+        compiler_params=pltpu.CompilerParams(
+            collective_id=1, has_side_effects=True, vmem_limit_bytes=63 << 20
+        ),
+        name="fused_experts",
+    )(ids, seats, y, scale, w_gate, w_up, w_down)
+
+
 def shards(
     queries,
     key_rows,
@@ -493,18 +802,20 @@
     scale = jnp.concatenate([weights, inverse[:, None, :]], axis=1)
     scale = jnp.pad(scale, ((0, 0), (0, 8 - scale.shape[1]), (0, 0)))
     scale = jnp.swapaxes(scale, 1, 2)
-    parts, grad_gate, grad_up, grad_down = experts(
-        order,
-        ids,
-        y_all,
-        scale,
-        jnp.swapaxes(w_gate, 1, 2),
-        jnp.swapaxes(w_up, 1, 2),
-        w_down,
-    )
+    weights_here = (jnp.swapaxes(w_gate, 1, 2), jnp.swapaxes(w_up, 1, 2), w_down)
+    if group_count == 4:
+        listed = own_cols - group_index * EXP_GROUP
+        same = listed[:, :, None] == jnp.arange(EXP_GROUP, dtype=jnp.int32)
+        place = jnp.arange(per_owner, dtype=jnp.int32)[None, :, None] - per_owner
+        seats = per_owner + jnp.sum(jnp.where(same, place, 0), axis=1)
+        sums, grad_gate, grad_up, grad_down = fused_experts(
+            listed.reshape(-1), seats.reshape(-1), y_all, scale, *weights_here, hidden_count
+        )
+    else:
+        parts, grad_gate, grad_up, grad_down = experts(order, ids, y_all, scale, *weights_here)
+        sums = reduce_parts(parts, 1)
     grad_gate = jnp.swapaxes(grad_gate, 1, 2)
     grad_up = jnp.swapaxes(grad_up, 1, 2)
-    sums = reduce_parts(parts, 1)
     layer_out = (stream + sums[0].astype(jnp.float32)).astype(jnp.bfloat16)
     return (layer_out, sums[1], grad_gate, grad_up, grad_down)
 

time: 234 us -> 211 us (0.902)
  Pallas kernels: 199 us -> 181 us
  matrix products: 7.67 us -> 4.4 us
    pallas_call x2 -> x1, Pallas kernels: 87.2 us -> 21.8 us  [reduce_parts(): pl.pallas_call(functools.partial(reduce_kernel, groups, hidden), out_shap...]
    pallas_call x1, Pallas kernels: 48.7 us -> 95.5 us  [fused_experts(): pl.pallas_call(functools.partial(fused_kernel, groups, hidden, per_owner)...]
    unnamed x7 -> x14, local copies, waits for them, and re-layouts: 6.28 us -> 9.3 us
where the time goes in v2:
time: 211 us
  Pallas kernels  181 us (86%)
  local copies, waits for them, and re-layouts  18.1 us (9%)
  other arithmetic  6.65 us (3%)
  matrix products  4.4 us (2%)
    pallas_call x1, Pallas kernels, fused_experts(): pl.pallas_call(functools.partial(fused_kernel, groups, hidden, per_owner)...  95.5 us
    pallas_call x1, Pallas kernels, gather_all(): pl.pallas_call(functools.partial(gather_kernel, groups, hidden), out_shap...  63.2 us
    pallas_call x1, Pallas kernels, reduce_parts(): pl.pallas_call(functools.partial(reduce_kernel, groups, hidden), out_shap...  21.8 us
    unnamed x14, local copies, waits for them, and re-layouts  9.3 us

profile of v2, /device:TPU:0, one launch (start us, length us, event | category | flops | bytes accessed | tf_op | source)
XLA Modules:
  0.0 210.5 jit_solution(2456812894444285665)
XLA Ops:
  0.6 0.0 copy-start
  0.7 0.8 dynamic_slice.28
  1.5 0.8 dynamic-slice_subtract_fusion
  2.2 0.6 reshape.99.ids_ref
  2.8 0.1 select_reduce_fusion.1
  2.9 0.6 add.77.seat_ref
  3.5 0.8 select_reduce_fusion
  4.4 1.6 constant_dynamic-slice_fusion.1
  6.1 1.9 fusion.39
  8.0 1.4 convolution_convert_fusion.1
  9.5 0.2 copy-done.3
  9.7 1.0 convolution_convert_fusion
  10.7 1.0 copy.44
  11.7 0.8 copy.45
  12.5 0.0 copy-start.4
  12.5 21.8 %reduce_parts_2.1 = bf16[1,384,256]{2,1,0:T(8,128)(2,1)S(1)} custom-call(bf16[1,8,1,384,256]{4,3,2,1,0:T(8,128)(2,1)S(1)} %bitcast.87), custom_call_target="tpu_custom_call" | custom-call | tf_op jit(solution)/shard_map/reduce_parts_2/pallas_call | solution.py:338
  34.3 1.1 multiply_convert_fusion
  35.5 0.8 pad_maximum_fusion.y_ref
  36.3 63.2 %gather_all.1.y_ref = bf16[4,8,2,400,256]{4,3,2,1,0:T(8,128)(2,1)} custom-call(bf16[2,400,256]{2,1,0:T(8,128)(2,1)} %pad_maximum_fusion.y_ref), custom_call_target="tpu_custom_call" | custom-call | tf_op jit(solution)/shard_map/gather_all/pallas_call | solution.py:216
  99.5 1.1 fusion.38
  100.6 0.1 reshape_squeeze.6
  100.8 0.1 reshape_squeeze.7
  101.0 0.3 copy.50
  101.3 0.3 copy.47
  101.6 1.2 fusion.5.scale_ref
  102.8 95.5 %fused_experts.1 = (bf16[2,384,256]{2,1,0:T(8,128)(2,1)}, bf16[8,96,2048]{2,1,0:T(8,128)(2,1)}, bf16[8,96,2048]{2,1,0:T(8,128)(2,1)}, bf16[8,96,2048]{2,1,0:T(8,128)(2,1)}) custom-call(s32[16]{0:T(128)} %reshape.99.ids_ref, s32[32]{0:T(128)} %add.77.seat_ref, bf16[4,8,2,400,256]{4,3,2,1,0:T(8,128)(2,1)} %gather_all.1.y_ref, f32[4,384,8]{2,1,0:T(8,128)} %fusion.5.scale_ref, ...), custom_call_target="tpu_custom_call" | custom-call | tf_op jit(solution)/shard_map/fused_experts/pallas_call | solution.py:701
  198.3 1.8 fusion.9
  200.1 1.6 slice_bitcast_fusion
  201.7 4.1 %copy.67 = bf16[8,2048,96]{1,2,0:T(8,128)(2,1)} copy(bf16[8,2048,96]{1,2,0:T(8,128)(2,1)} %bitcast.90) | data formatting | bytes 6291456
  205.8 1.7 copy.68
  207.5 1.4 copy-done.1
  208.9 1.7 copy.69
  (27 shorter events, 0.3 us)
Async XLA Ops:
  0.6 5.4 %copy-start = (bf16[384,512]{1,0:T(8,128)(2,1)S(1)}, bf16[384,512]{1,0:T(8,128)(2,1)}, u32[]{:S(2)}) copy-start(bf16[384,512]{1,0:T(8,128)(2,1)} %param.14) | copy-start | bytes 1179652
  8.0 1.6 copy-start.3
  12.5 23.0 %copy-start.4 = (bf16[384,256]{1,0:T(8,128)(2,1)S(1)}, bf16[384,256]{1,0:T(8,128)(2,1)}, u32[]{:S(2)}) copy-start(bf16[384,256]{1,0:T(8,128)(2,1)} %constant_dynamic-slice_fusion.1) | copy-start | bytes 589828
  201.7 4.1 %copy-start.2 = (bf16[8,96,2048]{2,1,0:T(8,128)(2,1)S(1)}, bf16[8,96,2048]{2,1,0:T(8,128)(2,1)}, u32[]{:S(2)}) copy-start(bf16[8,96,2048]{2,1,0:T(8,128)(2,1)} %get-tuple-element.11) | copy-start | bytes 9437188
  205.8 3.0 %copy-start.1 = (bf16[8,96,2048]{2,1,0:T(8,128)(2,1)S(1)}, bf16[8,96,2048]{2,1,0:T(8,128)(2,1)}, u32[]{:S(2)}) copy-start(bf16[8,96,2048]{2,1,0:T(8,128)(2,1)} %get-tuple-element.36) | copy-start | bytes 9437188

commit v3 on v2

--- a/solution.py
+++ b/solution.py
@@ -441,9 +441,9 @@
     ids_ref, seat_ref, y_ref, scale_ref, gate_ref, up_ref, down_ref,
     out_ref, gate_out, up_out, down_out,
     w_gate, w_up, w_down, xs, cs, w_in, w_out, act, grads, act_turned, grads_turned,
-    slot_gate, slot_up, slot_down, acc_gate, acc_up, acc_down,
-    own, stage, pair_in, peer_in0, peer_in1, ring_in0, ring_in1,
-    load_sems, fetch_sems, pair_sems, ring1_sems, peer0_sems, peer1_sems, ring0_sems,
+    slot_gate, slot_up, slot_down,
+    own, stage, pair_in, diag_in, peer_in0, peer_in1, ring_in0, ring_in1,
+    load_sems, fetch_sems, pair_sems, ring1_sems, diag_sems, peer0_sems, peer1_sems, ring0_sems,
 ):
     g, h = lax.axis_index("group"), lax.axis_index("hidden")
     chips = hidden // 2
@@ -453,6 +453,7 @@
     last, final = chips - 1, groups - 1
     cut = first_rows(tokens)
     rows = (pl.ds(0, cut), pl.ds(cut, tokens - cut))
+    via = (pl.ds(0, cut // 2), pl.ds(cut // 2, cut // 2))
     ahead = {"group": g, "hidden": lax.rem(h + 2, hidden)}
     behind = {"group": g, "hidden": lax.rem(h + hidden - 2, hidden)}
     partner_h = h + 1 - 2 * lax.rem(h, 2)
@@ -473,7 +474,7 @@
     ]
     stores = [
         pltpu.make_async_copy(a, b, load_sems.at[n])
-        for n, (a, b) in enumerate(((acc_gate, gate_out), (acc_up, up_out), (acc_down, down_out)))
+        for n, (a, b) in enumerate(((w_gate, gate_out), (w_up, up_out), (w_down, down_out)))
     ]
 
     def fetches(i):
@@ -496,9 +497,6 @@
     for copy in loads:
         copy.start()
 
-    acc_gate[...] = jnp.zeros_like(acc_gate)
-    acc_up[...] = jnp.zeros_like(acc_up)
-    acc_down[...] = jnp.zeros_like(acc_down)
     for buffer in (slot_gate, slot_up, slot_down):
         buffer[per_owner] = jnp.zeros(buffer.shape[1:], buffer.dtype)
 
@@ -521,8 +519,12 @@
     def ring1_copy(i, t):
         return remote(part_of(i, t, 1), ring_in1.at[i, t], ring1_sems, (i, t), ahead)
 
+    def diag_copy(n, t):
+        source = own.at[0, t, :, via[n]]
+        return remote(source, diag_in.at[n, t], diag_sems, (n, t), peer(n + 1))
+
     def peer0_copy(i, t):
-        return remote(part_of(i, t, 0), peer_in0.at[i, t], peer0_sems, (i, t), peer(i))
+        return remote(part_of(i, t, 0), peer_in0.at[i - 1, t], peer0_sems, (i - 1, t), peer(i))
 
     def peer1_copy(i):
         return remote(part_of(i, 0, 1), peer_in1.at[i], peer1_sems, (i,), peer(i))
@@ -544,9 +546,18 @@
         def _():
             ring1_copy(i, t).start()
 
-        @pl.when(i < final)
+        @pl.when(i == 0)
         def _():
-            peer0_copy(i, t).start()
+            for n in range(2):
+                diag_copy(n, t).start()
+
+        for n, step in ((1, 1), (0, 2)):
+
+            @pl.when(i == step)
+            def _():
+                diag_copy(n, t).wait_recv()
+                add(own.at[step, t, :, via[n]], diag_in.at[n, t])
+                peer0_copy(step, t).start()
 
     def ring_task(i, t):
         before = t - 1 if t else last
@@ -557,9 +568,9 @@
 
     def finish_task(t):
         arrived = []
-        for i in range(final):
+        for i in range(1, final):
             peer0_copy(i, t).wait_recv()
-            arrived.append(peer_in0.at[i, t])
+            arrived.append(peer_in0.at[i - 1, t])
         if t != 1:
             before = t - 1 if t else last
             ring0_copy(before).wait_recv()
@@ -608,9 +619,18 @@
         act[...] = weighted.astype(act.dtype)
         grads[:, :half] = d_gate.astype(grads.dtype)
         grads[:, half:] = d_up.astype(grads.dtype)
-        act_turned[...] = act[...].T
-        grads_turned[:half, :] = (d_gate * inverse).astype(grads.dtype).T
-        grads_turned[half:, :] = (d_up * inverse).astype(grads.dtype).T
+        act_turned[i] = act[...].T
+        grads_turned[i, :half, :] = (d_gate * inverse).astype(grads.dtype).T
+        grads_turned[i, half:, :] = (d_up * inverse).astype(grads.dtype).T
+
+        @pl.when(i > 0)
+        def _():
+            ring_task(i - 1, 2)
+
+        @pl.when(i > 1)
+        def _():
+            ring_task(i - 2, 0)
+            peer1_copy(i - 2).start()
 
         @pl.loop(0, chips)
         def _(j):
@@ -628,53 +648,81 @@
             def _():
                 pair_task(i, j)
 
-            @pl.when((i > 0) & (j == 1))
-            def _():
-                ring_task(i - 1, 0)
-                peer1_copy(i - 1).start()
-
         pair_task(i, 0)
-        ring_task(i, 2)
-
-        @pl.when(i == final)
+
+        @pl.when(i > 0)
         def _():
-            finish_task(1)
-
-        @pl.loop(0, hidden)
-        def _(b):
-            cols = pl.ds(pl.multiple_of(b * width, width), width)
-            down = dot(act_turned[...], cs[slot, :, cols])
-            both = dot(grads_turned[...], xs[slot, :, cols])
-            for s in range(per_owner):
-                slot_down[s] = down[s * units : (s + 1) * units]
-                slot_gate[s] = both[s * units : (s + 1) * units]
-                slot_up[s] = both[half + s * units : half + (s + 1) * units]
-            for e in range(owned):
-                seat = seat_ref[group * owned + e]
-                for total, value in ((acc_down, slot_down), (acc_gate, slot_gate), (acc_up, slot_up)):
-                    total[e, :, cols] = (total[e, :, cols].astype(jnp.float32) + value[seat]).astype(
-                        total.dtype
-                    )
-
-        ring_task(i, 3)
+            ring_task(i - 1, 3)
+
+    for buffer in (w_gate, w_up, w_down):
+        buffer[...] = jnp.zeros_like(buffer)
+
+    def finish_last():
+        for i in range(final):
+            peer1_copy(i).wait_recv()
+        add(part_of(final, 0, 1), *[peer_in1.at[i] for i in range(final)])
+
+    def finish_ring():
+        ring_task(final - 1, 0)
+        peer1_copy(final - 1).start()
+
+    tasks = (
+        (2, lambda: ring_task(final, 2)),
+        (3, lambda: finish_task(1)),
+        (6, finish_ring),
+        (9, lambda: ring_task(final, 3)),
+        (13, lambda: finish_task(2)),
+        (16, lambda: ring_task(final, 0)),
+        (23, lambda: finish_task(3)),
+    )
+
+    @pl.loop(0, groups * hidden)
+    def _(n):
+        i, b = final - n // hidden, lax.rem(n, hidden)
+        slot = lax.rem(i, 2)
+        group = pair_groups(g, i)
+
+        @pl.when((b == 0) & (n > 0) & (i > 0))
+        def _():
+            for copy in fetches(i - 1):
+                copy.start()
+
+        @pl.when((b == 0) & (i < final - 1))
+        def _():
+            for copy in fetches(i):
+                copy.wait()
+
+        cols = pl.ds(pl.multiple_of(b * width, width), width)
+        down = dot(act_turned[i], cs[slot, :, cols])
+        both = dot(grads_turned[i], xs[slot, :, cols])
+        for s in range(per_owner):
+            slot_down[s] = down[s * units : (s + 1) * units]
+            slot_gate[s] = both[s * units : (s + 1) * units]
+            slot_up[s] = both[half + s * units : half + (s + 1) * units]
+        for e in range(owned):
+            seat = seat_ref[group * owned + e]
+            for total, value in ((w_down, slot_down), (w_gate, slot_gate), (w_up, slot_up)):
+                total[e, :, cols] = (total[e, :, cols].astype(jnp.float32) + value[seat]).astype(
+                    total.dtype
+                )
+        for at, task in tasks:
+            pl.when(n == at)(task)
 
     for copy in stores:
         copy.start()
-    finish_task(2)
-    ring_task(final, 0)
-    finish_task(3)
     finish_task(0)
-    for i in range(final):
-        peer1_copy(i).wait_recv()
-    add(part_of(final, 0, 1), *[peer_in1.at[i] for i in range(final)])
+    finish_last()
     out_ref[...] = own[final, 0]
     for i in range(groups):
         for t in range(chips):
             pair_copy(i, t).wait_send()
             if t:
                 ring1_copy(i, t).wait_send()
-            if i < final:
+            if 0 < i < final:
                 peer0_copy(i, t).wait_send()
+    for t in range(chips):
+        for n in range(2):
+            diag_copy(n, t).wait_send()
     for i in range(final):
         peer1_copy(i).wait_send()
     for t in range(1, chips):
@@ -711,16 +759,16 @@
             pltpu.VMEM((half, model), bf),
             pltpu.VMEM((tokens, half), bf),
             pltpu.VMEM((tokens, 2 * half), bf),
-            pltpu.VMEM((half, tokens), bf),
-            pltpu.VMEM((2 * half, tokens), bf),
+            pltpu.VMEM((groups, half, tokens), bf),
+            pltpu.VMEM((groups, 2 * half, tokens), bf),
         ]
         + [pltpu.VMEM((per_owner + 1, units, width), jnp.float32)] * 3
-        + [pltpu.VMEM(w_down.shape, bf)] * 3
         + [
             pltpu.VMEM((groups, chips) + block, bf),
             pltpu.VMEM((groups, chips) + block, bf),
             pltpu.VMEM((groups, chips) + block, bf),
-            pltpu.VMEM((groups - 1, chips) + first, bf),
+            pltpu.VMEM((2, chips, 2, cut // 2, width), bf),
+            pltpu.VMEM((groups - 2, chips) + first, bf),
             pltpu.VMEM((groups - 1,) + second, bf),
             pltpu.VMEM((chips,) + first, bf),
             pltpu.VMEM((groups, chips) + second, bf),
@@ -728,7 +776,8 @@
             dma((2, 2, hidden)),
             dma((2, groups, chips)),
             dma((2, groups, chips)),
-            dma((2, groups - 1, chips)),
+            dma((2, 2, chips)),
+            dma((2, groups - 2, chips)),
             dma((2, groups - 1)),
             dma((2, chips)),
         ],

time: 211 us -> 196 us (0.929)
  Pallas kernels: 181 us -> 166 us
    pallas_call x1, Pallas kernels: 95.5 us -> 80.6 us  [fused_experts(): pl.pallas_call(functools.partial(fused_kernel, groups, hidden, per_owner)...]
where the time goes in v3:
time: 196 us
  Pallas kernels  166 us (85%)
  local copies, waits for them, and re-layouts  18.1 us (9%)
  other arithmetic  6.65 us (3%)
  matrix products  4.4 us (2%)
    pallas_call x1, Pallas kernels, fused_experts(): pl.pallas_call(functools.partial(fused_kernel, groups, hidden, per_owner)...  80.6 us
    pallas_call x1, Pallas kernels, gather_all(): pl.pallas_call(functools.partial(gather_kernel, groups, hidden), out_shap...  63.2 us
    pallas_call x1, Pallas kernels, reduce_parts(): pl.pallas_call(functools.partial(reduce_kernel, groups, hidden), out_shap...  21.8 us
    unnamed x14, local copies, waits for them, and re-layouts  9.3 us

profile of v3, /device:TPU:0, one launch (start us, length us, event | category | flops | bytes accessed | tf_op | source)
XLA Modules:
  0.0 195.6 jit_solution(4520897619070527063)
XLA Ops:
  0.6 0.0 copy-start
  0.7 0.8 dynamic_slice.28
  1.5 0.8 dynamic-slice_subtract_fusion
  2.2 0.6 reshape.99.ids_ref
  2.8 0.1 select_reduce_fusion.1
  2.9 0.6 add.77.seat_ref
  3.5 0.8 select_reduce_fusion
  4.4 1.6 constant_dynamic-slice_fusion.1
  6.1 1.9 fusion.39
  8.0 1.4 convolution_convert_fusion.1
  9.5 0.2 copy-done.3
  9.7 1.0 convolution_convert_fusion
  10.7 1.0 copy.44
  11.7 0.8 copy.45
  12.5 0.0 copy-start.4
  12.5 21.8 %reduce_parts_2.1 = bf16[1,384,256]{2,1,0:T(8,128)(2,1)S(1)} custom-call(bf16[1,8,1,384,256]{4,3,2,1,0:T(8,128)(2,1)S(1)} %bitcast.87), custom_call_target="tpu_custom_call" | custom-call | tf_op jit(solution)/shard_map/reduce_parts_2/pallas_call | solution.py:338
  34.3 1.1 multiply_convert_fusion
  35.5 0.8 pad_maximum_fusion.y_ref
  36.3 63.2 %gather_all.1.y_ref = bf16[4,8,2,400,256]{4,3,2,1,0:T(8,128)(2,1)} custom-call(bf16[2,400,256]{2,1,0:T(8,128)(2,1)} %pad_maximum_fusion.y_ref), custom_call_target="tpu_custom_call" | custom-call | tf_op jit(solution)/shard_map/gather_all/pallas_call | solution.py:216
  99.5 1.1 fusion.38
  100.6 0.1 reshape_squeeze.6
  100.8 0.1 reshape_squeeze.7
  101.0 0.3 copy.50
  101.3 0.3 copy.47
  101.6 1.2 fusion.5.scale_ref
  102.8 80.6 %fused_experts.1 = (bf16[2,384,256]{2,1,0:T(8,128)(2,1)}, bf16[8,96,2048]{2,1,0:T(8,128)(2,1)}, bf16[8,96,2048]{2,1,0:T(8,128)(2,1)}, bf16[8,96,2048]{2,1,0:T(8,128)(2,1)}) custom-call(s32[16]{0:T(128)} %reshape.99.ids_ref, s32[32]{0:T(128)} %add.77.seat_ref, bf16[4,8,2,400,256]{4,3,2,1,0:T(8,128)(2,1)} %gather_all.1.y_ref, f32[4,384,8]{2,1,0:T(8,128)} %fusion.5.scale_ref, ...), custom_call_target="tpu_custom_call" | custom-call | tf_op jit(solution)/shard_map/fused_experts/pallas_call | solution.py:749
  183.4 1.8 fusion.9
  185.1 1.6 slice_bitcast_fusion
  186.8 4.1 %copy.67 = bf16[8,2048,96]{1,2,0:T(8,128)(2,1)} copy(bf16[8,2048,96]{1,2,0:T(8,128)(2,1)} %bitcast.90) | data formatting | bytes 6291456
  190.9 1.7 copy.68
  192.5 1.4 copy-done.1
  193.9 1.7 copy.69
  (27 shorter events, 0.3 us)
Async XLA Ops:
  0.6 5.4 %copy-start = (bf16[384,512]{1,0:T(8,128)(2,1)S(1)}, bf16[384,512]{1,0:T(8,128)(2,1)}, u32[]{:S(2)}) copy-start(bf16[384,512]{1,0:T(8,128)(2,1)} %param.14) | copy-start | bytes 1179652
  8.0 1.6 copy-start.3
  12.5 23.0 %copy-start.4 = (bf16[384,256]{1,0:T(8,128)(2,1)S(1)}, bf16[384,256]{1,0:T(8,128)(2,1)}, u32[]{:S(2)}) copy-start(bf16[384,256]{1,0:T(8,128)(2,1)} %constant_dynamic-slice_fusion.1) | copy-start | bytes 589828
  186.8 4.1 %copy-start.2 = (bf16[8,96,2048]{2,1,0:T(8,128)(2,1)S(1)}, bf16[8,96,2048]{2,1,0:T(8,128)(2,1)}, u32[]{:S(2)}) copy-start(bf16[8,96,2048]{2,1,0:T(8,128)(2,1)} %get-tuple-element.11) | copy-start | bytes 9437188
  190.9 3.0 %copy-start.1 = (bf16[8,96,2048]{2,1,0:T(8,128)(2,1)S(1)}, bf16[8,96,2048]{2,1,0:T(8,128)(2,1)}, u32[]{:S(2)}) copy-start(bf16[8,96,2048]{2,1,0:T(8,128)(2,1)} %get-tuple-element.36) | copy-start | bytes 9437188

commit v4 on v3

--- a/solution.py
+++ b/solution.py
@@ -436,9 +436,176 @@
     return lax.rem(gy + along, 2) * 2 + lax.rem(gx + across, 2)
 
 
+def front_kernel(
+    groups, hidden, q_ref, k_ref, v_ref, proj_ref, cot_ref, slot_ref,
+    out_ref, cot_all, slot_all,
+    mixed, own, stage, pair_in, ring_in,
+    local_sem, slot_sems, cot_sems, pair_sems, ring_sems,
+):
+    g, h = lax.axis_index("group"), lax.axis_index("hidden")
+    chips = hidden // 2
+    last, final = chips - 1, groups - 1
+    tokens, width = out_ref.shape
+    heads_here = q_ref.shape[1] // HEAD_DIM
+    ahead = {"group": g, "hidden": lax.rem(h + 2, hidden)}
+    behind = {"group": g, "hidden": lax.rem(h + hidden - 2, hidden)}
+    partner_h = h + 1 - 2 * lax.rem(h, 2)
+    partner = {"group": g, "hidden": partner_h}
+    mesh_id = pl.DeviceIdType.MESH
+    source = [pair_groups(g, i) for i in range(groups)]
+    peers = [{"group": source[i], "hidden": h} for i in range(final)]
+
+    barrier = pltpu.get_barrier_semaphore()
+    greeted = [ahead, behind, partner] + peers
+    for device in greeted:
+        pl.semaphore_signal(barrier, inc=1, device_id=device, device_id_type=mesh_id)
+    pl.semaphore_wait(barrier, len(greeted))
+
+    def remote(source_ref, target, sems, index, device):
+        return pltpu.make_async_remote_copy(
+            src_ref=source_ref,
+            dst_ref=target,
+            send_sem=sems.at[(0,) + index],
+            recv_sem=sems.at[(1,) + index],
+            device_id=device,
+            device_id_type=mesh_id,
+        )
+
+    quarter = tokens // 4
+    base = lax.rem(h, 2) * (2 * quarter)
+
+    def piece(n):
+        return pl.ds(pl.multiple_of(base + n * quarter, quarter), quarter)
+
+    def landed(i, n):
+        return cot_all.at[source[i], piece(n)]
+
+    made = {}
+
+    def send(key, source_ref, target, device):
+        copy = remote(source_ref, target, cot_sems, (len(made),), device)
+        copy.start()
+        made[key] = copy
+
+    for i, n in ((1, 0), (2, 1), (1, 1), (2, 0)):
+        send(("near", i, n), cot_ref.at[piece(n)], cot_all.at[g, piece(n)], peers[i])
+    slots = [remote(slot_ref, slot_all.at[g], slot_sems, (i,), peers[i]) for i in range(final)]
+    for copy in slots:
+        copy.start()
+    local = pltpu.make_async_copy(cot_ref, cot_all.at[g], local_sem)
+    local.start()
+    slot_all[g] = slot_ref[...]
+
+    def pass_on(i, n, forward):
+        made["far" if i == 0 else "near", i, n].wait_recv()
+        if forward:
+            send(("far", 0, n), landed(i, n), landed(i, n), peers[3 - i])
+        send(("pair", i, n), landed(i, n), landed(i, n), partner)
+
+    kv = h * heads_here // (HEADS // KV_HEADS)
+    kv_cols = pl.ds(pl.multiple_of(kv * HEAD_DIM, HEAD_DIM), HEAD_DIM)
+    keys, values = k_ref[:, kv_cols], v_ref[:, kv_cols]
+    seen = lax.broadcasted_iota(jnp.int32, (tokens, tokens), 0) >= lax.broadcasted_iota(
+        jnp.int32, (tokens, tokens), 1
+    )
+    for head in range(heads_here):
+        cols = slice(head * HEAD_DIM, (head + 1) * HEAD_DIM)
+        scores = dot(q_ref[:, cols], keys, ((1,), (1,))) / math.sqrt(HEAD_DIM)
+        scores = jnp.where(seen, scores, -1e30)
+        weights = jnp.exp(scores - jnp.max(scores, axis=-1, keepdims=True))
+        total = jnp.sum(weights, axis=-1, keepdims=True)
+        mixed[:, cols] = dot((weights / total).astype(mixed.dtype), values).astype(mixed.dtype)
+
+    def pair_copy(t):
+        return remote(stage.at[t], pair_in.at[t], pair_sems, (t,), partner)
+
+    def ring_copy(t):
+        return remote(own.at[t], ring_in.at[t], ring_sems, (t,), ahead)
+
+    def add(into, *others):
+        total = into[...].astype(jnp.float32)
+        for other in others:
+            total = total + other[...].astype(jnp.float32)
+        into[...] = total.astype(into.dtype)
+
+    def reduce_task(t):
+        pair_copy(t).wait_recv()
+        if t == 1:
+            add(own.at[t], pair_in.at[t])
+        else:
+            before = t - 1 if t else last
+            ring_copy(before).wait_recv()
+            add(own.at[t], pair_in.at[t], ring_in.at[before])
+        if t:
+            ring_copy(t).start()
+
+    @pl.loop(0, chips)
+    def _(j):
+        t = lax.rem(j + 1, chips)
+        for whose, target in ((partner_h, stage), (h, own)):
+            first = pl.multiple_of(lax.rem(whose + hidden - 2 * t, hidden) * width, width)
+            target[t] = dot(mixed[...], proj_ref[:, pl.ds(first, width)]).astype(target.dtype)
+            if whose is partner_h:
+                pair_copy(t).start()
+
+        @pl.when(j == 1)
+        def _():
+            reduce_task(1)
+
+    pass_on(1, 0, True)
+    pass_on(2, 1, True)
+    for t in list(range(2, chips)) + [0]:
+        reduce_task(t)
+        if t == 2:
+            pass_on(1, 1, False)
+            pass_on(2, 0, False)
+    pass_on(0, 0, False)
+    pass_on(0, 1, False)
+    out_ref[...] = own[0]
+    for key, copy in made.items():
+        if key[0] == "pair":
+            copy.wait_recv()
+        copy.wait_send()
+    for copy in slots:
+        copy.wait()
+    for t in range(chips):
+        pair_copy(t).wait_send()
+        if t:
+            ring_copy(t).wait_send()
+    local.wait()
+
+
+def front(queries, key_rows, value_rows, out_proj, cotangent, slots, groups, hidden):
+    tokens, model = cotangent.shape
+    width = model // hidden
+    chips = hidden // 2
+    bf = queries.dtype
+    vmem = pl.BlockSpec(memory_space=pltpu.VMEM)
+    dma = pltpu.SemaphoreType.DMA
+    block = pltpu.VMEM((chips, tokens, width), bf)
+    return pl.pallas_call(
+        functools.partial(front_kernel, groups, hidden),
+        in_specs=[vmem] * 6,
+        out_specs=[vmem, pl.BlockSpec(memory_space=pl.ANY), vmem],
+        out_shape=[
+            jax.ShapeDtypeStruct((tokens, width), bf),
+            jax.ShapeDtypeStruct((groups,) + cotangent.shape, bf),
+            jax.ShapeDtypeStruct((groups,) + slots.shape, slots.dtype),
+        ],
+        scratch_shapes=[
+            pltpu.VMEM(queries.shape, bf), block, block, block, block,
+            dma, dma((2, groups - 1)), dma((2, 12)), dma((2, chips)), dma((2, chips)),
+        ],
+        compiler_params=pltpu.CompilerParams(
+            collective_id=2, has_side_effects=True, vmem_limit_bytes=40 << 20
+        ),
+        name="front",
+    )(queries, key_rows, value_rows, out_proj, cotangent, slots)
+
+
 def fused_kernel(
     groups, hidden, per_owner,
-    ids_ref, seat_ref, y_ref, scale_ref, gate_ref, up_ref, down_ref,
+    ids_ref, seat_ref, y_ref, cot_ref, scale_ref, gate_ref, up_ref, down_ref,
     out_ref, gate_out, up_out, down_out,
     w_gate, w_up, w_down, xs, cs, w_in, w_out, act, grads, act_turned, grads_turned,
     slot_gate, slot_up, slot_down,
@@ -480,16 +647,17 @@
     def fetches(i):
         slot = lax.rem(i, 2)
         source = pair_groups(g, i)
-        copies = []
+        copies = [
+            pltpu.make_async_copy(cot_ref.at[source], cs.at[slot], fetch_sems.at[slot, hidden])
+        ]
         for b in range(hidden):
-            for p, target in enumerate((xs, cs)):
-                copies.append(
-                    pltpu.make_async_copy(
-                        y_ref.at[source, b, p, pl.ds(0, tokens)],
-                        target.at[slot, :, pl.ds(b * width, width)],
-                        fetch_sems.at[slot, p, b],
-                    )
+            copies.append(
+                pltpu.make_async_copy(
+                    y_ref.at[source, b, 0, pl.ds(0, tokens)],
+                    xs.at[slot, :, pl.ds(b * width, width)],
+                    fetch_sems.at[slot, b],
                 )
+            )
         return copies
 
     for copy in fetches(0):
@@ -731,7 +899,7 @@
         copy.wait()
 
 
-def fused_experts(ids, seats, y, scale, w_gate, w_up, w_down, hidden):
+def fused_experts(ids, seats, y, cot, scale, w_gate, w_up, w_down, hidden):
     groups = y.shape[0]
     width = y.shape[4]
     tokens = scale.shape[1]
@@ -748,7 +916,8 @@
     dma = pltpu.SemaphoreType.DMA
     return pl.pallas_call(
         functools.partial(fused_kernel, groups, hidden, per_owner),
-        in_specs=[scalars, scalars, anywhere, pl.BlockSpec(memory_space=pltpu.VMEM)] + [anywhere] * 3,
+        in_specs=[scalars, scalars, anywhere, anywhere, pl.BlockSpec(memory_space=pltpu.VMEM)]
+        + [anywhere] * 3,
         out_specs=[pl.BlockSpec(memory_space=pltpu.VMEM)] + [anywhere] * 3,
         out_shape=[jax.ShapeDtypeStruct(block, bf)] + [jax.ShapeDtypeStruct(w_down.shape, bf)] * 3,
         scratch_shapes=[pltpu.VMEM(w_down.shape, bf)] * 3
@@ -773,7 +942,7 @@
             pltpu.VMEM((chips,) + first, bf),
             pltpu.VMEM((groups, chips) + second, bf),
             dma((3,)),
-            dma((2, 2, hidden)),
+            dma((2, hidden + 1)),
             dma((2, groups, chips)),
             dma((2, groups, chips)),
             dma((2, 2, chips)),
@@ -785,7 +954,7 @@
             collective_id=1, has_side_effects=True, vmem_limit_bytes=63 << 20
         ),
         name="fused_experts",
-    )(ids, seats, y, scale, w_gate, w_up, w_down)
+    )(ids, seats, y, cot, scale, w_gate, w_up, w_down)
 
 
 def shards(
@@ -812,20 +981,26 @@
 
     chosen = route_slot[:, :, None] == jnp.arange(FETCH, dtype=jnp.int32)[None, None, :]
     slot_weight = jnp.sum(jnp.where(chosen, route_weight[:, :, None], 0.0), axis=1)
-    order = (group_index + jnp.arange(group_count, dtype=jnp.int32)) % group_count
     own_cols = lax.dynamic_slice_in_dim(fetch_list, group_index * per_owner, per_owner, 1)
-    ids = jnp.take(own_cols - group_index * EXP_GROUP, order, axis=0)
-
+    listed = own_cols - group_index * EXP_GROUP
     heads_here = queries.shape[1] // HEAD_DIM
-    kv_index = hidden_index * heads_here // (HEADS // KV_HEADS)
-    key_block = lax.dynamic_slice_in_dim(key_rows, kv_index * HEAD_DIM, HEAD_DIM, 1)
-    value_block = lax.dynamic_slice_in_dim(value_rows, kv_index * HEAD_DIM, HEAD_DIM, 1)
-    mixed = attention_rows(queries, key_block, value_block, heads_here)
-    partial_value = jnp.dot(mixed, out_proj, preferred_element_type=jnp.float32)
     share_width = model // hidden_count
     first_col = hidden_index * share_width
-    blocks = partial_value.astype(jnp.bfloat16).reshape(tokens_here, hidden_count, share_width)
-    attn_share = reduce_parts(jnp.swapaxes(blocks, 0, 1)[None, :, None], 2)[0]
+    weights_here = (jnp.swapaxes(w_gate, 1, 2), jnp.swapaxes(w_up, 1, 2), w_down)
+    fused = group_count == 4
+    if fused:
+        attn_share, cot_all, slot_all = front(
+            queries, key_rows, value_rows, out_proj, cotangent, slot_weight.T,
+            group_count, hidden_count,
+        )
+    else:
+        kv_index = hidden_index * heads_here // (HEADS // KV_HEADS)
+        key_block = lax.dynamic_slice_in_dim(key_rows, kv_index * HEAD_DIM, HEAD_DIM, 1)
+        value_block = lax.dynamic_slice_in_dim(value_rows, kv_index * HEAD_DIM, HEAD_DIM, 1)
+        mixed = attention_rows(queries, key_block, value_block, heads_here)
+        partial_value = jnp.dot(mixed, out_proj, preferred_element_type=jnp.float32)
+        blocks = partial_value.astype(jnp.bfloat16).reshape(tokens_here, hidden_count, share_width)
+        attn_share = reduce_parts(jnp.swapaxes(blocks, 0, 1)[None, :, None], 2)[0]
     stream = lax.dynamic_slice_in_dim(residual, first_col, share_width, 1).astype(
         jnp.float32
     ) + attn_share.astype(jnp.float32)
@@ -833,34 +1008,36 @@
     squares = jnp.sum(stream * stream, axis=-1)
     gained = (stream * gain).astype(jnp.bfloat16)
     slots_here = FETCH // hidden_count
-    slots = lax.dynamic_slice_in_dim(slot_weight.T, hidden_index * slots_here, slots_here, 0)
     extra = -(-3 * slots_here * tokens_here // (16 * share_width)) * 16
-    cot_share = lax.dynamic_slice_in_dim(cotangent, first_col, share_width, 1)
-    y = jnp.stack(
-        [
-            jnp.concatenate([gained, to_rows(squares, extra, share_width)]),
-            jnp.concatenate([cot_share, to_rows(slots, extra, share_width)]),
-        ]
-    )
+    y = jnp.concatenate([gained, to_rows(squares, extra, share_width)])[None]
+    if not fused:
+        slots = lax.dynamic_slice_in_dim(slot_weight.T, hidden_index * slots_here, slots_here, 0)
+        cot_share = lax.dynamic_slice_in_dim(cotangent, first_col, share_width, 1)
+        y = jnp.concatenate(
+            [y, jnp.concatenate([cot_share, to_rows(slots, extra, share_width)])[None]]
+        )
     y_all = gather_all(y, group_count, hidden_count)
     squares_all = from_rows(y_all[:, :, 0, tokens_here:], tokens_here).sum(axis=1)
     inverse = lax.rsqrt(squares_all / model + epsilon)
-    weights = from_rows(y_all[:, :, 1, tokens_here:], slots_here * tokens_here)
-    weights = weights.reshape(group_count, FETCH, tokens_here)
+    if fused:
+        weights = slot_all
+    else:
+        weights = from_rows(y_all[:, :, 1, tokens_here:], slots_here * tokens_here)
+        weights = weights.reshape(group_count, FETCH, tokens_here)
     weights = lax.dynamic_slice_in_dim(weights, group_index * per_owner, per_owner, 1)
     scale = jnp.concatenate([weights, inverse[:, None, :]], axis=1)
     scale = jnp.pad(scale, ((0, 0), (0, 8 - scale.shape[1]), (0, 0)))
     scale = jnp.swapaxes(scale, 1, 2)
-    weights_here = (jnp.swapaxes(w_gate, 1, 2), jnp.swapaxes(w_up, 1, 2), w_down)
-    if group_count == 4:
-        listed = own_cols - group_index * EXP_GROUP
+    if fused:
         same = listed[:, :, None] == jnp.arange(EXP_GROUP, dtype=jnp.int32)
         place = jnp.arange(per_owner, dtype=jnp.int32)[None, :, None] - per_owner
         seats = per_owner + jnp.sum(jnp.where(same, place, 0), axis=1)
         sums, grad_gate, grad_up, grad_down = fused_experts(
-            listed.reshape(-1), seats.reshape(-1), y_all, scale, *weights_here, hidden_count
+            listed.reshape(-1), seats.reshape(-1), y_all, cot_all, scale, *weights_here, hidden_count
         )
     else:
+        order = (group_index + jnp.arange(group_count, dtype=jnp.int32)) % group_count
+        ids = jnp.take(listed, order, axis=0)
         parts, grad_gate, grad_up, grad_down = experts(order, ids, y_all, scale, *weights_here)
         sums = reduce_parts(parts, 1)
     grad_gate = jnp.swapaxes(grad_gate, 1, 2)

time: 196 us -> 185 us (0.944)
  Pallas kernels: 166 us -> 154 us
  local copies, waits for them, and re-layouts: 18.1 us -> 23 us
  matrix products: 4.4 us -> 0 us
    pallas_call x1, Pallas kernels: 63.2 us -> 37.2 us  [gather_all(): pl.pallas_call(functools.partial(gather_kernel, groups, hidden), out_shap...]
    pallas_call x1, Pallas kernels: 21.8 us -> 35.7 us  [front(): pl.pallas_call(functools.partial(front_kernel, groups, hidden), in_specs=...]
    unnamed x14 -> x19, local copies, waits for them, and re-layouts: 9.3 us -> 17.4 us
    dot_general x2 -> x0, matrix products: 2.45 us -> none  [the longest x1 1.45 us: attention_rows(): jnp.einsum('hts,sd->thd', probabilities, value_block, preferred_element_t...]
where the time goes in v4:
time: 185 us; the launch traced here: 184 us
  Pallas kernels  154 us (83%)
  local copies, waits for them, and re-layouts  23 us (12%)
  other arithmetic  6.4 us (3%)
    pallas_call x1, Pallas kernels, fused_experts(): pl.pallas_call(functools.partial(fused_kernel, groups, hidden, per_owner)...  81.4 us
    pallas_call x1, Pallas kernels, gather_all(): pl.pallas_call(functools.partial(gather_kernel, groups, hidden), out_shap...  37.2 us
    pallas_call x1, Pallas kernels, front(): pl.pallas_call(functools.partial(front_kernel, groups, hidden), in_specs=...  35.7 us
    unnamed x19, local copies, waits for them, and re-layouts  17.4 us

profile of v4, /device:TPU:0, one launch (start us, length us, event | category | flops | bytes accessed | tf_op | source)
XLA Modules:
  0.0 184.3 jit_solution(659064428269650570)
XLA Ops:
  0.6 0.8 dynamic_slice.14
  1.4 0.8 dynamic-slice_subtract_fusion
  2.2 0.6 reshape.75.ids_ref
  2.8 0.1 select_reduce_fusion.1
  2.9 0.6 add.59.seat_ref
  3.5 0.8 select_reduce_fusion
  4.2 0.0 copy-start.1
  4.2 1.6 copy-done.1
  5.8 1.4 copy-done.2
  7.2 1.0 copy-done.3
  8.2 1.0 copy-done.4
  9.2 1.0 copy-done.5
  10.2 35.7 %front.1 = (bf16[384,256]{1,0:T(8,128)(2,1)S(1)}, bf16[4,384,2048]{2,1,0:T(8,128)(2,1)S(1)}, f32[4,16,384]{2,1,0:T(8,128)S(1)}) custom-call(bf16[384,512]{1,0:T(8,128)(2,1)S(1)} %copy-done.3, bf16[384,512]{1,0:T(8,128)(2,1)S(1)} %copy-done.4, bf16[384,512]{1,0:T(8,128)(2,1)S(1)} %copy-done.5, bf16[512,2048]{1,0:T(8,128)(2,1)S(1)} %copy-done.1, ...), custom_call_target="tpu_custom_call" | custom-call | tf_op jit(solution)/shard_map/front/pallas_call | solution.py:586
  45.9 0.0 copy-start
  45.9 2.6 %copy-done = bf16[4,384,2048]{2,1,0:T(8,128)(2,1)} copy-done((bf16[4,384,2048]{2,1,0:T(8,128)(2,1)}, bf16[4,384,2048]{2,1,0:T(8,128)(2,1)S(1)}, u32[]{:S(2)}) %copy-start) | copy-done | bytes 6291480
  48.5 1.1 multiply_convert_fusion
  49.7 0.7 maximum_bitcast_fusion.y_ref
  50.4 0.3 copy.29
  50.7 0.3 constant_dynamic-slice_fusion
  50.9 37.2 %gather_all.1.y_ref = bf16[4,8,1,400,256]{4,3,2,1,0:T(8,128)(2,1)} custom-call(bf16[1,400,256]{2,1,0:T(8,128)(2,1)} %maximum_bitcast_fusion.y_ref), custom_call_target="tpu_custom_call" | custom-call | tf_op jit(solution)/shard_map/gather_all/pallas_call | solution.py:216
  88.1 1.0 slice.21
  89.1 0.1 reshape_squeeze.3
  89.3 0.3 copy.30
  89.6 1.2 fusion.scale_ref
  90.8 81.4 %fused_experts.1 = (bf16[2,384,256]{2,1,0:T(8,128)(2,1)}, bf16[8,96,2048]{2,1,0:T(8,128)(2,1)}, bf16[8,96,2048]{2,1,0:T(8,128)(2,1)}, bf16[8,96,2048]{2,1,0:T(8,128)(2,1)}) custom-call(s32[16]{0:T(128)} %reshape.75.ids_ref, s32[32]{0:T(128)} %add.59.seat_ref, bf16[4,8,1,400,256]{4,3,2,1,0:T(8,128)(2,1)} %gather_all.1.y_ref, bf16[4,384,2048]{2,1,0:T(8,128)(2,1)} %copy-done, ...), custom_call_target="tpu_custom_call" | custom-call | tf_op jit(solution)/shard_map/fused_experts/pallas_call | solution.py:917
  172.1 1.8 fusion.1
  173.9 1.6 slice_bitcast_fusion
  175.5 4.1 %copy.34 = bf16[8,2048,96]{1,2,0:T(8,128)(2,1)} copy(bf16[8,2048,96]{1,2,0:T(8,128)(2,1)} %bitcast.20) | data formatting | bytes 6291456
  179.6 0.0 copy-done.7
  179.6 1.7 copy.35
  181.3 1.4 copy-done.6
  182.7 1.7 copy.36
  (16 shorter events, 0.1 us)
Async XLA Ops:
  4.2 1.6 copy-start.1
  5.8 1.4 copy-start.2
  7.2 1.0 copy-start.3
  8.2 1.0 copy-start.4
  9.2 1.0 copy-start.5
  45.9 2.6 %copy-start = (bf16[4,384,2048]{2,1,0:T(8,128)(2,1)}, bf16[4,384,2048]{2,1,0:T(8,128)(2,1)S(1)}, u32[]{:S(2)}) copy-start(bf16[4,384,2048]{2,1,0:T(8,128)(2,1)S(1)} %get-tuple-element.13.cot_ref) | copy-start | bytes 18874372
  175.5 4.1 %copy-start.7 = (bf16[8,96,2048]{2,1,0:T(8,128)(2,1)S(1)}, bf16[8,96,2048]{2,1,0:T(8,128)(2,1)}, u32[]{:S(2)}) copy-start(bf16[8,96,2048]{2,1,0:T(8,128)(2,1)} %get-tuple-element.17) | copy-start | bytes 9437188
  179.6 3.0 %copy-start.6 = (bf16[8,96,2048]{2,1,0:T(8,128)(2,1)S(1)}, bf16[8,96,2048]{2,1,0:T(8,128)(2,1)}, u32[]{:S(2)}) copy-start(bf16[8,96,2048]{2,1,0:T(8,128)(2,1)} %get-tuple-element.33) | copy-start | bytes 9437188

commit v5 on v1

--- a/solution.py
+++ b/solution.py
@@ -430,6 +430,629 @@
     )
 
 
+def pair_groups(g, i):
+    across, along = 1 - i // 2, 1 - lax.rem(i, 2)
+    gx, gy = lax.rem(g, 2), g // 2
+    return lax.rem(gy + along, 2) * 2 + lax.rem(gx + across, 2)
+
+
+def near_rows(count):
+    return count // 40 * 32
+
+
+def layer_kernel(
+    groups, hidden,
+    fetch_ref, q_ref, k_ref, v_ref, proj_ref, cot_ref, res_ref, gain_ref, seats_ref, shares_ref,
+    gate_ref, up_ref, down_ref,
+    layer_out, normed_out, w_gate, w_up, w_down, cot_all, x_all,
+    q, k, v, proj, residual, mixed, f_own, f_stage, f_pair, f_ring, stream, y, slot_rows, slot_all,
+    xs, cs, tails, w_in, w_out, act, grads, act_turned, grads_turned, slot_gate, slot_up, slot_down,
+    own, stage, pair_in, diag_in, peer_in0, peer_in1, ring_in0, ring_in1,
+    load_sems, slot_sems, cot_sems, f_pair_sems, f_ring_sems, y_sems, fetch_sems,
+    pair_sems, ring1_sems, diag_sems, peer0_sems, peer1_sems, ring0_sems,
+):
+    g, h = lax.axis_index("group"), lax.axis_index("hidden")
+    chips = hidden // 2
+    owned, units, model = w_gate.shape
+    tokens, width = layer_out.shape
+    per_owner = fetch_ref.shape[1] // groups
+    half = per_owner * units
+    last, final = chips - 1, groups - 1
+    turns = list(range(1, chips)) + [0]
+    ahead = {"group": g, "hidden": lax.rem(h + 2, hidden)}
+    behind = {"group": g, "hidden": lax.rem(h + hidden - 2, hidden)}
+    partner_h = h + 1 - 2 * lax.rem(h, 2)
+    partner = {"group": g, "hidden": partner_h}
+    mesh_id = pl.DeviceIdType.MESH
+    source = [pair_groups(g, i) for i in range(groups)]
+    peers = [{"group": source[i], "hidden": h} for i in range(final)]
+    turned = ((1,), (1,))
+
+    barrier = pltpu.get_barrier_semaphore()
+    greeted = [ahead, behind, partner] + peers
+    for device in greeted:
+        pl.semaphore_signal(barrier, inc=1, device_id=device, device_id_type=mesh_id)
+
+    my_cols = pl.ds(pl.multiple_of(h * width, width), width)
+    moves = (
+        (q_ref, q), (k_ref, k), (v_ref, v), (proj_ref, proj), (res_ref.at[:, my_cols], residual),
+        (gate_ref, w_gate), (up_ref, w_up), (down_ref, w_down),
+    )
+    loads = [pltpu.make_async_copy(a, b, load_sems.at[n]) for n, (a, b) in enumerate(moves)]
+    for copy in loads:
+        copy.start()
+
+    slot_rows[...] = jnp.zeros_like(slot_rows)
+    for f in range(groups * per_owner):
+        named = jnp.where(seats_ref[...] == f, shares_ref[...], 0.0)
+        slot_rows[f // per_owner, f % per_owner : f % per_owner + 1, :] = jnp.sum(
+            named, axis=0, keepdims=True
+        )
+    for buffer in (slot_gate, slot_up, slot_down):
+        buffer[per_owner] = jnp.zeros(buffer.shape[1:], buffer.dtype)
+    slot_all[g] = slot_rows[g]
+
+    def remote(source_ref, target, sems, index, device):
+        return pltpu.make_async_remote_copy(
+            src_ref=source_ref,
+            dst_ref=target,
+            send_sem=sems.at[(0,) + index],
+            recv_sem=sems.at[(1,) + index],
+            device_id=device,
+            device_id_type=mesh_id,
+        )
+
+    def add(into, *others):
+        total = into[...].astype(jnp.float32)
+        for other in others:
+            total = total + other[...].astype(jnp.float32)
+        into[...] = total.astype(into.dtype)
+
+    pl.semaphore_wait(barrier, len(greeted))
+
+    quarter = tokens // 4
+    base = lax.rem(h, 2) * (2 * quarter)
+    cot_made = {}
+
+    def piece(n):
+        return pl.ds(pl.multiple_of(base + n * quarter, quarter), quarter)
+
+    def landed(i, n):
+        return cot_all.at[source[i], piece(n)]
+
+    def send_cot(key, source_ref, target, device):
+        copy = remote(source_ref, target, cot_sems, (len(cot_made),), device)
+        copy.start()
+        cot_made[key] = copy
+
+    for i, n in ((1, 0), (2, 1), (1, 1), (2, 0)):
+        send_cot(("near", i, n), cot_ref.at[piece(n)], cot_all.at[g, piece(n)], peers[i])
+    slots = [
+        remote(slot_rows.at[source[i]], slot_all.at[g], slot_sems, (i,), peers[i])
+        for i in range(final)
+    ]
+    for copy in slots:
+        copy.start()
+
+    def pass_cot(i, n, forward):
+        cot_made["far" if i == 0 else "near", i, n].wait_recv()
+        if forward:
+            send_cot(("far", 0, n), landed(i, n), landed(i, n), peers[3 - i])
+        send_cot(("pair", i, n), landed(i, n), landed(i, n), partner)
+
+    for copy in loads[:3]:
+        copy.wait()
+    heads_here = q.shape[1] // HEAD_DIM
+    kv = h * heads_here // (HEADS // KV_HEADS)
+    kv_cols = pl.ds(pl.multiple_of(kv * HEAD_DIM, HEAD_DIM), HEAD_DIM)
+    keys, values = k[:, kv_cols], v[:, kv_cols]
+    seen = lax.broadcasted_iota(jnp.int32, (tokens, tokens), 0) >= lax.broadcasted_iota(
+        jnp.int32, (tokens, tokens), 1
+    )
+    for head in range(heads_here):
+        cols = slice(head * HEAD_DIM, (head + 1) * HEAD_DIM)
+        scores = dot(q[:, cols], keys, turned) / math.sqrt(HEAD_DIM)
+        scores = jnp.where(seen, scores, -1e30)
+        weights = jnp.exp(scores - jnp.max(scores, axis=-1, keepdims=True))
+        total = jnp.sum(weights, axis=-1, keepdims=True)
+        mixed[:, cols] = dot((weights / total).astype(mixed.dtype), values).astype(mixed.dtype)
+
+    def f_pair_copy(t):
+        return remote(f_stage.at[t], f_pair.at[t], f_pair_sems, (t,), partner)
+
+    def f_ring_copy(t):
+        return remote(f_own.at[t], f_ring.at[t], f_ring_sems, (t,), ahead)
+
+    def reduce_task(t):
+        f_pair_copy(t).wait_recv()
+        if t == 1:
+            add(f_own.at[t], f_pair.at[t])
+        else:
+            before = t - 1 if t else last
+            f_ring_copy(before).wait_recv()
+            add(f_own.at[t], f_pair.at[t], f_ring.at[before])
+        if t:
+            f_ring_copy(t).start()
+
+    for copy in loads[3:5]:
+        copy.wait()
+
+    @pl.loop(0, chips)
+    def _(j):
+        t = lax.rem(j + 1, chips)
+        for whose, target in ((partner_h, f_stage), (h, f_own)):
+            first = pl.multiple_of(lax.rem(whose + hidden - 2 * t, hidden) * width, width)
+            target[t] = dot(mixed[...], proj[:, pl.ds(first, width)]).astype(target.dtype)
+            if whose is partner_h:
+                f_pair_copy(t).start()
+
+        @pl.when(j == 1)
+        def _():
+            reduce_task(1)
+
+    pass_cot(1, 0, True)
+    pass_cot(2, 1, True)
+    for t in turns[1:]:
+        reduce_task(t)
+        if t == 2:
+            pass_cot(1, 1, False)
+            pass_cot(2, 0, False)
+
+    stream[...] = residual[...].astype(jnp.float32) + f_own[0].astype(jnp.float32)
+    y[:tokens, :] = (stream[...] * gain_ref[:, my_cols]).astype(y.dtype)
+    squares = jnp.sum(stream[...] * stream[...], axis=-1, keepdims=True)
+    squares = jnp.broadcast_to(squares, (tokens, 128)).T[:16]
+    high = squares.astype(y.dtype).astype(jnp.float32)
+    middle = (squares - high).astype(y.dtype).astype(jnp.float32)
+    low = squares - high - middle
+    row = lax.broadcasted_iota(jnp.int32, (16, width), 0)
+    extras = jnp.zeros((16, width), jnp.float32)
+    for c in range(-(-tokens // width)):
+        count = min(width, tokens - c * width)
+        for n, term in enumerate((high, middle, low)):
+            term = term[:, c * width : c * width + count]
+            if count < width:
+                term = jnp.concatenate([term, jnp.zeros((16, width - count), jnp.float32)], axis=1)
+            extras = jnp.where(row == 3 * c + n, term, extras)
+    y[tokens:, :] = extras.astype(y.dtype)
+
+    rows_all = y.shape[0]
+    near = near_rows(rows_all)
+    spans = {0: pl.ds(0, near), 1: pl.ds(near, rows_all - near)}
+    spans["a"], spans["b"] = pl.ds(0, near // 2), pl.ds(near // 2, near // 2)
+    behind_h = [lax.rem(h + hidden - 2 * t, hidden) for t in range(chips)]
+    y_made = {}
+
+    def send_y(key, mine, i, t, span, device):
+        target = x_all.at[source[i], behind_h[t], spans[span]]
+        copy = remote(
+            y.at[spans[span]] if mine else target, target, y_sems, (len(y_made),), device
+        )
+        copy.start()
+        y_made[key] = copy
+
+    home = groups - 1
+
+    def ring_y0(t):
+        y_made["ring0", t].wait_recv()
+        if t + 1 < chips:
+            send_y(("ring0", t + 1), False, home, t, 0, ahead)
+        for i in (1, 2):
+            send_y(("near0", t, i), False, home, t, 0, peers[i])
+        send_y(("pair", home, t, 0), False, home, t, 0, partner)
+
+    def ring_y1(t, i):
+        y_made["ring1", t, i].wait_recv()
+        if t + 1 < chips:
+            send_y(("ring1", t + 1, i), False, i, t, 1, ahead)
+        send_y(("pair", i, t, 1), False, i, t, 1, partner)
+
+    def near_y0(t):
+        for i, span in ((1, "a"), (2, "b")):
+            y_made["near0", t, i].wait_recv()
+            send_y(("far0", t, span), False, i, t, span, peers[3 - i])
+            send_y(("pair", i, t, 0), False, i, t, 0, partner)
+
+    def far_y0(t):
+        for span in ("a", "b"):
+            y_made["far0", t, span].wait_recv()
+            send_y(("pair", 0, t, span), False, 0, t, span, partner)
+
+    local = pltpu.make_async_copy(y, x_all.at[g, h], load_sems.at[len(moves)])
+    local.start()
+    send_y(("ring0", 1), True, home, 0, 0, ahead)
+    for i in (1, 2):
+        send_y(("near0", 0, i), True, home, 0, 0, peers[i])
+    for i in (1, 2, 0):
+        send_y(("near1", i), True, home, 0, 1, peers[i])
+    send_y(("ring1", 1, home), True, home, 0, 1, ahead)
+    for span in (0, 1):
+        send_y(("pair", home, 0, span), True, home, 0, span, partner)
+    pass_cot(0, 0, False)
+    pass_cot(0, 1, False)
+    ring_y0(1)
+    near_y0(0)
+    for i in (1, 2, 0):
+        y_made["near1", i].wait_recv()
+        send_y(("ring1", 1, i), False, i, 0, 1, ahead)
+        send_y(("pair", i, 0, 1), False, i, 0, 1, partner)
+    ring_y1(1, home)
+    for t in range(2, chips):
+        ring_y0(t)
+        near_y0(t - 1)
+        far_y0(t - 2)
+        for i in range(final):
+            ring_y1(t - 1, i)
+        ring_y1(t, home)
+    near_y0(last)
+    far_y0(last - 1)
+    for i in range(final):
+        ring_y1(last, i)
+    far_y0(last)
+    local.wait()
+    for made in (cot_made, y_made):
+        for key, copy in made.items():
+            if key[0] == "pair":
+                copy.wait_recv()
+            copy.wait_send()
+    for copy in slots:
+        copy.wait()
+    for t in turns:
+        f_pair_copy(t).wait_send()
+        if t:
+            f_ring_copy(t).wait_send()
+    for copy in loads[5:]:
+        copy.wait()
+
+    cut = first_rows(tokens)
+    rows = (pl.ds(0, cut), pl.ds(cut, tokens - cut))
+    via = (pl.ds(0, cut // 2), pl.ds(cut // 2, cut // 2))
+
+    def peer(i):
+        return {"group": pair_groups(g, i), "hidden": h}
+
+    def fetch_x(i):
+        slot = lax.rem(i, 2)
+        group = pair_groups(g, i)
+        copies = []
+        for b in range(hidden):
+            cols = pl.ds(b * width, width)
+            copies.append(
+                pltpu.make_async_copy(
+                    x_all.at[group, b, pl.ds(0, tokens)], xs.at[slot, :, cols], fetch_sems.at[slot, b]
+                )
+            )
+            copies.append(
+                pltpu.make_async_copy(
+                    x_all.at[group, b, pl.ds(tokens, 16)],
+                    tails.at[slot, :, cols],
+                    fetch_sems.at[slot, hidden + b],
+                )
+            )
+        return copies
+
+    def fetch_c(i, mine):
+        slot = lax.rem(i, 2)
+        origin = cot_ref if mine else cot_all.at[pair_groups(g, i)]
+        return pltpu.make_async_copy(origin, cs.at[slot], fetch_sems.at[slot, 2 * hidden])
+
+    def start_fetch(i):
+        for copy in fetch_x(i):
+            copy.start()
+
+        @pl.when(i < final)
+        def _():
+            fetch_c(i, False).start()
+
+        @pl.when(i == final)
+        def _():
+            fetch_c(i, True).start()
+
+    def wait_fetch(i):
+        for copy in fetch_x(i):
+            copy.wait()
+        fetch_c(i, False).wait()
+
+    def part_of(i, t, part):
+        return own.at[i, t, :, rows[part]]
+
+    def pair_copy(i, t):
+        return remote(stage.at[lax.rem(i, 2), t], pair_in.at[i, t], pair_sems, (i, t), partner)
+
+    def ring1_copy(i, t):
+        return remote(part_of(i, t, 1), ring_in1.at[i, t], ring1_sems, (i, t), ahead)
+
+    def diag_copy(n, t):
+        return remote(own.at[0, t, :, via[n]], diag_in.at[n, t], diag_sems, (n, t), peer(n + 1))
+
+    def peer0_copy(i, t):
+        return remote(part_of(i, t, 0), peer_in0.at[i - 1, t], peer0_sems, (i - 1, t), peer(i))
+
+    def peer1_copy(i):
+        return remote(part_of(i, 0, 1), peer_in1.at[i], peer1_sems, (i,), peer(i))
+
+    def ring0_copy(t):
+        return remote(part_of(final, t, 0), ring_in0.at[t], ring0_sems, (t,), ahead)
+
+    def pair_task(i, t):
+        pair_copy(i, t).wait_recv()
+        add(own.at[i, t], pair_in.at[i, t])
+        if t == 1:
+            ring1_copy(i, t).start()
+
+        @pl.when(i == 0)
+        def _():
+            for n in range(2):
+                diag_copy(n, t).start()
+
+        for n, step in ((1, 1), (0, 2)):
+
+            @pl.when(i == step)
+            def _():
+                diag_copy(n, t).wait_recv()
+                add(own.at[step, t, :, via[n]], diag_in.at[n, t])
+                peer0_copy(step, t).start()
+
+    def ring_task(i, t):
+        before = t - 1 if t else last
+        ring1_copy(i, before).wait_recv()
+        add(part_of(i, t, 1), ring_in1.at[i, before])
+        if t:
+            ring1_copy(i, t).start()
+
+    def finish_task(t):
+        arrived = []
+        for i in range(1, final):
+            peer0_copy(i, t).wait_recv()
+            arrived.append(peer_in0.at[i - 1, t])
+        if t != 1:
+            before = t - 1 if t else last
+            ring0_copy(before).wait_recv()
+            arrived.append(ring_in0.at[before])
+        add(part_of(final, t, 0), *arrived)
+        if t:
+            ring0_copy(t).start()
+
+    def finish_ring(i):
+        ring_task(i, 0)
+        peer1_copy(i).start()
+
+    def scale_of(slot, group):
+        terms = jnp.zeros((16, width), jnp.float32)
+        for b in range(hidden):
+            terms = terms + tails[slot, :, b * width : (b + 1) * width].astype(jnp.float32)
+        chunks = []
+        for c in range(-(-tokens // width)):
+            count = min(width, tokens - c * width)
+            total = terms[3 * c : 3 * c + 1] + terms[3 * c + 1 : 3 * c + 2] + terms[3 * c + 2 : 3 * c + 3]
+            chunks.append(total[:, :count])
+        inverse = lax.rsqrt(jnp.concatenate(chunks, axis=1) / model + epsilon)
+        row = lax.broadcasted_iota(jnp.int32, (8, tokens), 0)
+        both = jnp.where(row == per_owner, inverse, slot_all[group])
+        return jnp.concatenate([both, jnp.zeros((120, tokens), jnp.float32)], axis=0).T
+
+    start_fetch(0)
+
+    @pl.loop(0, groups)
+    def _(i):
+        slot = lax.rem(i, 2)
+        group = pair_groups(g, i)
+
+        @pl.when(i > 0)
+        def _():
+            pair_task(i - 1, 1)
+
+        @pl.when(i < final)
+        def _():
+            start_fetch(i + 1)
+
+        for s in range(per_owner):
+            e = lax.rem(fetch_ref[group, g * per_owner + s], owned)
+            w_in[s * units : (s + 1) * units, :] = w_gate[e]
+            w_in[half + s * units : half + (s + 1) * units, :] = w_up[e]
+            w_out[s * units : (s + 1) * units, :] = w_down[e]
+        wait_fetch(i)
+        scale = scale_of(slot, group)
+        inverse = scale[:, per_owner : per_owner + 1]
+        lane = lax.broadcasted_iota(jnp.int32, (tokens, half), 1)
+        weight = jnp.broadcast_to(scale[:, :1], (tokens, half))
+        for s in range(1, per_owner):
+            weight = jnp.where(lane >= s * units, scale[:, s : s + 1], weight)
+        pre_gate = dot(xs[slot], w_in[:half, :], turned) * inverse
+
+        @pl.when(i > 0)
+        def _():
+            pair_task(i - 1, 2)
+
+        pre_up = dot(xs[slot], w_in[half:, :], turned) * inverse
+
+        @pl.when(i > 0)
+        def _():
+            pair_task(i - 1, 3)
+
+        @pl.when(i > 1)
+        def _():
+            ring_task(i - 2, 3)
+
+        d_act = dot(cs[slot], w_out[...], turned) * weight
+
+        @pl.when(i > 0)
+        def _():
+            pair_task(i - 1, 0)
+
+        sig = jax.nn.sigmoid(pre_gate)
+        swish = pre_gate * sig
+        weighted = swish * pre_up * weight
+        d_gate = d_act * pre_up * sig * (1.0 + pre_gate * (1.0 - sig))
+        d_up = d_act * swish
+        act[...] = weighted.astype(act.dtype)
+        grads[:, :half] = d_gate.astype(grads.dtype)
+        grads[:, half:] = d_up.astype(grads.dtype)
+        act_turned[i] = act[...].T
+        grads_turned[i, :half, :] = (d_gate * inverse).astype(grads.dtype).T
+        grads_turned[i, half:, :] = (d_up * inverse).astype(grads.dtype).T
+
+        @pl.loop(0, chips)
+        def _(j):
+            t = lax.rem(j + 1, chips)
+
+            @pl.when(i > 1)
+            def _():
+                pair_copy(i - 2, t).wait_send()
+
+            for whose, target, at in ((partner_h, stage, slot), (h, own, i)):
+                first = pl.multiple_of(lax.rem(whose + hidden - 2 * t, hidden) * width, width)
+                cols = pl.ds(first, width)
+                target[at, t, 0] = dot(act[...], w_out[:, cols]).astype(target.dtype)
+                target[at, t, 1] = dot(grads[...], w_in[:, cols]).astype(target.dtype)
+                if whose is partner_h:
+                    pair_copy(i, t).start()
+
+        @pl.when(i > 0)
+        def _():
+            ring_task(i - 1, 2)
+
+        @pl.when(i > 1)
+        def _():
+            finish_ring(i - 2)
+
+    for buffer in (w_gate, w_up, w_down):
+        buffer[...] = jnp.zeros_like(buffer)
+
+    tasks = (
+        (0, lambda: pair_task(final, 1)),
+        (1, lambda: pair_task(final, 2)),
+        (3, lambda: pair_task(final, 3)),
+        (4, lambda: ring_task(final - 1, 3)),
+        (5, lambda: pair_task(final, 0)),
+        (6, lambda: finish_task(1)),
+        (9, lambda: ring_task(final, 2)),
+        (12, lambda: finish_ring(final - 1)),
+        (15, lambda: finish_task(2)),
+        (18, lambda: ring_task(final, 3)),
+        (25, lambda: finish_task(3)),
+        (27, lambda: ring_task(final, 0)),
+    )
+
+    @pl.loop(0, groups * hidden)
+    def _(n):
+        i, b = final - n // hidden, lax.rem(n, hidden)
+        slot = lax.rem(i, 2)
+        group = pair_groups(g, i)
+
+        @pl.when((b == 0) & (n > 0) & (i > 0))
+        def _():
+            start_fetch(i - 1)
+
+        @pl.when((b == 0) & (i < final - 1))
+        def _():
+            wait_fetch(i)
+
+        cols = pl.ds(pl.multiple_of(b * width, width), width)
+        down = dot(act_turned[i], cs[slot, :, cols])
+        both = dot(grads_turned[i], xs[slot, :, cols])
+        for s in range(per_owner):
+            slot_down[s] = down[s * units : (s + 1) * units]
+            slot_gate[s] = both[s * units : (s + 1) * units]
+            slot_up[s] = both[half + s * units : half + (s + 1) * units]
+        listed = [lax.rem(fetch_ref[group, g * per_owner + s], owned) for s in range(per_owner)]
+        for e in range(owned):
+            seat = jnp.int32(per_owner)
+            for s in range(per_owner):
+                seat = jnp.where(listed[s] == e, s, seat)
+            for total, value in ((w_down, slot_down), (w_gate, slot_gate), (w_up, slot_up)):
+                total[e, :, cols] = (total[e, :, cols].astype(jnp.float32) + value[seat]).astype(
+                    total.dtype
+                )
+        for at, task in tasks:
+            pl.when(n == at)(task)
+
+    finish_task(0)
+    for i in range(final):
+        peer1_copy(i).wait_recv()
+    add(part_of(final, 0, 1), *[peer_in1.at[i] for i in range(final)])
+    layer_out[...] = (stream[...] + own[final, 0, 0].astype(jnp.float32)).astype(layer_out.dtype)
+    normed_out[...] = own[final, 0, 1]
+    for t in range(chips):
+        for i in range(groups):
+            if i + 2 >= groups:
+                pair_copy(i, t).wait_send()
+            if t:
+                ring1_copy(i, t).wait_send()
+            if 0 < i < final:
+                peer0_copy(i, t).wait_send()
+        for n in range(2):
+            diag_copy(n, t).wait_send()
+        if t:
+            ring0_copy(t).wait_send()
+    for i in range(final):
+        peer1_copy(i).wait_send()
+
+
+def layer(
+    fetch_list, queries, key_rows, value_rows, out_proj, cotangent, residual, gain, seats, shares,
+    w_gate, w_up, w_down, groups, hidden,
+):
+    tokens, model = cotangent.shape
+    width = model // hidden
+    chips = hidden // 2
+    owned, units, _ = w_down.shape
+    per_owner = fetch_list.shape[1] // groups
+    half = per_owner * units
+    bf = queries.dtype
+    cut = first_rows(tokens)
+    block = (2, tokens, width)
+    vmem = pl.BlockSpec(memory_space=pltpu.VMEM)
+    anywhere = pl.BlockSpec(memory_space=pl.ANY)
+    dma = pltpu.SemaphoreType.DMA
+    f32 = jnp.float32
+    shape = jax.ShapeDtypeStruct
+    scratch = [
+        (queries.shape, bf), (key_rows.shape, bf), (value_rows.shape, bf), (out_proj.shape, bf),
+        ((tokens, width), bf), (queries.shape, bf)
+    ]
+    scratch += [((chips, tokens, width), bf)] * 4
+    scratch += [
+        ((tokens, width), f32), ((tokens + 16, width), bf),
+        ((groups, 8, tokens), f32), ((groups, 8, tokens), f32),
+        ((2, tokens, model), bf), ((2, tokens, model), bf), ((2, 16, model), bf),
+        ((2 * half, model), bf), ((half, model), bf), ((tokens, half), bf), ((tokens, 2 * half), bf),
+        ((groups, half, tokens), bf), ((groups, 2 * half, tokens), bf),
+    ]
+    scratch += [((per_owner + 1, units, width), f32)] * 3
+    scratch += [
+        ((groups, chips) + block, bf), ((2, chips) + block, bf), ((groups, chips) + block, bf),
+        ((2, chips, 2, cut // 2, width), bf),
+        ((groups - 2, chips, 2, cut, width), bf), ((groups - 1, 2, tokens - cut, width), bf),
+        ((chips, 2, cut, width), bf), ((groups, chips, 2, tokens - cut, width), bf),
+    ]
+    sems = [
+        (9,), (2, groups - 1), (2, 12), (2, chips), (2, chips), (2, 72), (2, 2 * hidden + 1),
+        (2, groups, chips), (2, groups, chips), (2, 2, chips), (2, groups - 2, chips),
+        (2, groups - 1), (2, chips),
+    ]
+    return pl.pallas_call(
+        functools.partial(layer_kernel, groups, hidden),
+        in_specs=[pl.BlockSpec(memory_space=pltpu.SMEM)]
+        + [anywhere] * 6 + [vmem] * 3 + [anywhere] * 3,
+        out_specs=[vmem] * 5 + [anywhere] * 2,
+        out_shape=[shape((tokens, width), bf)] * 2
+        + [shape(w_down.shape, bf)] * 3
+        + [
+            shape((groups, tokens, model), bf),
+            shape((groups, hidden, tokens + 16, width), bf),
+        ],
+        scratch_shapes=[pltpu.VMEM(*s) for s in scratch] + [dma(s) for s in sems],
+        compiler_params=pltpu.CompilerParams(
+            collective_id=1, has_side_effects=True, vmem_limit_bytes=61 << 20
+        ),
+        name="layer",
+    )(
+        fetch_list, queries, key_rows, value_rows, out_proj, cotangent, residual, gain, seats,
+        shares, w_gate, w_up, w_down,
+    )
+
+
 def shards(
     queries,
     key_rows,
@@ -451,6 +1074,17 @@
     group_index = lax.axis_index("group")
     group_count = lax.axis_size("group")
     per_owner = FETCH // group_count
+
+    if group_count == 4:
+        outs = layer(
+            fetch_list, queries, key_rows, value_rows, out_proj, cotangent, residual,
+            norm_gain[None], route_slot.T, route_weight.T,
+            jnp.swapaxes(w_gate, 1, 2), jnp.swapaxes(w_up, 1, 2), w_down,
+            group_count, hidden_count,
+        )
+        return (
+            outs[0], outs[1], jnp.swapaxes(outs[2], 1, 2), jnp.swapaxes(outs[3], 1, 2), outs[4]
+        )
 
     chosen = route_slot[:, :, None] == jnp.arange(FETCH, dtype=jnp.int32)[None, None, :]
     slot_weight = jnp.sum(jnp.where(chosen, route_weight[:, :, None], 0.0), axis=1)

time: 234 us -> 154 us (0.66)
  Pallas kernels: 199 us -> 141 us
  other arithmetic: 8.37 us -> 0 us
  matrix products: 7.67 us -> 0 us
  local copies, waits for them, and re-layouts: 17.2 us -> 12 us
    pallas_call x4 -> x1, Pallas kernels: 199 us -> 141 us  [layer(): pl.pallas_call(functools.partial(layer_kernel, groups, hidden), in_specs=...]
    unnamed x7 -> x9, local copies, waits for them, and re-layouts: 6.28 us -> 12 us
    dot_general x2 -> x0, matrix products: 4.29 us -> none  [the longest x1 2.16 us: shards(): partial_value = jnp.dot(mixed, out_proj, preferred_element_type=jnp.float32)]
    sub x1 -> x0, matrix products: 3.37 us -> none  [attention_rows(): weights = jnp.exp(scores - row_peak)]
    convert_element_type x4 -> x0, other arithmetic: 2.82 us -> none  [the longest x1 1.68 us: shards(): layer_out = (stream + sums[0].astype(jnp.float32)).astype(jnp.bfloat16)]
    convert_element_type x3 -> x0, local copies, waits for them, and re-layouts: 2.61 us -> none  [the longest x1 2.58 us: shards(): partial_value.astype(jnp.bfloat16)]
    reshape x4 -> x0, local copies, waits for them, and re-layouts: 2.61 us -> none  [the longest x1 2.57 us: shards(): partial_value.astype(jnp.bfloat16)]
    transpose x1 -> x0, other arithmetic: 2.36 us -> none  [shards(): scale = jnp.swapaxes(scale, 1, 2)]
where the time goes in v5:
time: 154 us
  Pallas kernels  141 us (92%)
  local copies, waits for them, and re-layouts  12 us (8%)
    pallas_call x1, Pallas kernels, layer(): pl.pallas_call(functools.partial(layer_kernel, groups, hidden), in_specs=...  141 us
    unnamed x9, local copies, waits for them, and re-layouts  12 us

profile of v5, /device:TPU:0, one launch (start us, length us, event | category | flops | bytes accessed | tf_op | source)
XLA Modules:
  0.0 154.1 jit_solution(35868149990385714)
XLA Ops:
  0.6 141.4 %layer.1 = (bf16[384,256]{1,0:T(8,128)(2,1)}, bf16[384,256]{1,0:T(8,128)(2,1)}, bf16[8,96,2048]{2,1,0:T(8,128)(2,1)}, bf16[8,96,2048]{2,1,0:T(8,128)(2,1)}, bf16...) custom-call(s32[4,16]{1,0:T(4,128)} %fetch_ref.1, ...), custom_call_target="tpu_custom_call" | custom-call | tf_op jit(solution)/shard_map/layer/pallas_call | solution.py:1034
  142.1 1.6 %copy.23 = bf16[384,256]{1,0:T(8,128)(2,1)} copy(bf16[384,256]{1,0:T(8,128)(2,1)} %get-tuple-element.20) | data formatting | bytes 393216
  143.7 1.6 %copy.24 = bf16[384,256]{1,0:T(8,128)(2,1)} copy(bf16[384,256]{1,0:T(8,128)(2,1)} %get-tuple-element.21) | data formatting | bytes 393216
  145.3 0.0 copy-start.1
  145.3 4.1 %copy.25 = bf16[8,2048,96]{1,2,0:T(8,128)(2,1)} copy(bf16[8,2048,96]{1,2,0:T(8,128)(2,1)} %bitcast.8) | data formatting | bytes 6291456
  149.4 0.0 copy-done.1
  149.4 0.0 copy-start
  149.4 1.7 %copy.26 = bf16[8,2048,96]{1,2,0:T(8,128)(2,1)} copy(bf16[8,2048,96]{1,2,0:T(8,128)(2,1)S(1)} %bitcast.7) | data formatting | bytes 6291456
  151.1 1.4 copy-done
  152.4 1.7 %copy.27 = bf16[8,96,2048]{2,1,0:T(8,128)(2,1)} copy(bf16[8,96,2048]{2,1,0:T(8,128)(2,1)S(1)} %copy-done) | data formatting | bytes 6291456
Async XLA Ops:
  145.3 4.1 %copy-start.1 = (bf16[8,96,2048]{2,1,0:T(8,128)(2,1)S(1)}, bf16[8,96,2048]{2,1,0:T(8,128)(2,1)}, u32[]{:S(2)}) copy-start(bf16[8,96,2048]{2,1,0:T(8,128)(2,1)} %get-tuple-element.13) | copy-start | bytes 9437188
  149.4 3.0 %copy-start = (bf16[8,96,2048]{2,1,0:T(8,128)(2,1)S(1)}, bf16[8,96,2048]{2,1,0:T(8,128)(2,1)}, u32[]{:S(2)}) copy-start(bf16[8,96,2048]{2,1,0:T(8,128)(2,1)} %get-tuple-element.24) | copy-start | bytes 9437188

commit v6 on v5

--- a/solution.py
+++ b/solution.py
@@ -15,6 +15,7 @@
 FETCH = 16
 
 epsilon = 1e-06
+STORE_LIMIT = 4 << 20
 
 
 def attention_rows(query_in, key_block, value_block, heads_here):
@@ -987,6 +988,30 @@
             ring0_copy(t).wait_send()
     for i in range(final):
         peer1_copy(i).wait_send()
+
+
+def store_kernel(count, *refs):
+    sources, targets, sems = refs[:count], refs[count:-1], refs[-1]
+    copies = [
+        pltpu.make_async_copy(a, b, sems.at[n]) for n, (a, b) in enumerate(zip(sources, targets))
+    ]
+    for copy in copies:
+        copy.start()
+    for copy in copies:
+        copy.wait()
+
+
+def store(*values):
+    count = len(values)
+    return pl.pallas_call(
+        functools.partial(store_kernel, count),
+        in_specs=[pl.BlockSpec(memory_space=pltpu.VMEM)] * count,
+        out_specs=[pl.BlockSpec(memory_space=pl.ANY)] * count,
+        out_shape=[jax.ShapeDtypeStruct(value.shape, value.dtype) for value in values],
+        scratch_shapes=[pltpu.SemaphoreType.DMA((count,))],
+        compiler_params=pltpu.CompilerParams(vmem_limit_bytes=STORE_LIMIT),
+        name="store",
+    )(*values)
 
 
 def layer(
@@ -1036,15 +1061,15 @@
         in_specs=[pl.BlockSpec(memory_space=pltpu.SMEM)]
         + [anywhere] * 6 + [vmem] * 3 + [anywhere] * 3,
         out_specs=[vmem] * 5 + [anywhere] * 2,
-        out_shape=[shape((tokens, width), bf)] * 2
-        + [shape(w_down.shape, bf)] * 3
+        out_shape=[pltpu.VMEM((tokens, width), bf)] * 2
+        + [pltpu.VMEM(w_down.shape, bf)] * 3
         + [
             shape((groups, tokens, model), bf),
             shape((groups, hidden, tokens + 16, width), bf),
         ],
         scratch_shapes=[pltpu.VMEM(*s) for s in scratch] + [dma(s) for s in sems],
         compiler_params=pltpu.CompilerParams(
-            collective_id=1, has_side_effects=True, vmem_limit_bytes=61 << 20
+            collective_id=1, has_side_effects=True, vmem_limit_bytes=51 << 20
         ),
         name="layer",
     )(
@@ -1082,6 +1107,7 @@
             jnp.swapaxes(w_gate, 1, 2), jnp.swapaxes(w_up, 1, 2), w_down,
             group_count, hidden_count,
         )
+        outs = store(*outs[:5])
         return (
             outs[0], outs[1], jnp.swapaxes(outs[2], 1, 2), jnp.swapaxes(outs[3], 1, 2), outs[4]
         )

time: 154 us -> 143 us (0.929)
  local copies, waits for them, and re-layouts: 12 us -> 0 us
    unnamed x9 -> x0, local copies, waits for them, and re-layouts: 12 us -> none
    pallas_call x0 -> x1, Pallas kernels: none -> 3.91 us  [store(): pl.pallas_call(functools.partial(store_kernel, count), in_specs=[pl.Block...]
    pallas_call x1, Pallas kernels: 141 us -> 138 us  [layer(): pl.pallas_call(functools.partial(layer_kernel, groups, hidden), in_specs=...]
where the time goes in v6:
time: 143 us; the launch traced here: 142 us
  Pallas kernels  142 us (99%)
    pallas_call x1, Pallas kernels, layer(): pl.pallas_call(functools.partial(layer_kernel, groups, hidden), in_specs=...  138 us
    pallas_call x1, Pallas kernels, store(): pl.pallas_call(functools.partial(store_kernel, count), in_specs=[pl.Block...  3.91 us

profile of v6, /device:TPU:0, one launch (start us, length us, event | category | flops | bytes accessed | tf_op | source)
XLA Modules:
  0.0 142.3 jit_solution(1252938473021871573)
XLA Ops:
  0.6 137.7 %layer.1 = (bf16[384,256]{1,0:T(8,128)(2,1)S(1)}, bf16[384,256]{1,0:T(8,128)(2,1)S(1)}, bf16[8,96,2048]{2,1,0:T(8,128)(2,1)S(1)}, bf16[8,96,2048]{2,1,0:T(8,128)...) custom-call(s32[4,16]{1,0:T(4,128)} %fetch_ref.1, ...), custom_call_target="tpu_custom_call" | custom-call | tf_op jit(solution)/shard_map/layer/pallas_call | solution.py:1059
  138.4 3.9 %store.1 = (bf16[384,256]{1,0:T(8,128)(2,1)}, bf16[384,256]{1,0:T(8,128)(2,1)}, bf16[8,96,2048]{2,1,0:T(8,128)(2,1)}, bf16[8,96,2048]{2,1,0:T(8,128)(2,1)}, bf16[8,96,2048]{2,1,0:T(8,128)(2,1)}) custom-call(bf16[384,256]{1,0:T(8,128)(2,1)S(1)} %get-tuple-element.15.refs_0_, bf16[384,256]{1,0:T(8,128)(2,1)S(1)} %get-tuple-element.16.refs_1_, ...), custom_call_target="tpu_custom_call" | custom-call | tf_op jit(solution)/shard_map/store/pallas_call | solution.py:1006

commit v7 on v6

--- a/solution.py
+++ b/solution.py
@@ -438,7 +438,11 @@
 
 
 def near_rows(count):
-    return count // 40 * 32
+    return count // 36 * 32
+
+
+def direct_rows(count):
+    return count * 5 // 192 * 32
 
 
 def layer_kernel(
@@ -561,19 +565,25 @@
     def f_pair_copy(t):
         return remote(f_stage.at[t], f_pair.at[t], f_pair_sems, (t,), partner)
 
-    def f_ring_copy(t):
-        return remote(f_own.at[t], f_ring.at[t], f_ring_sems, (t,), ahead)
-
-    def reduce_task(t):
-        f_pair_copy(t).wait_recv()
+    middle_row = tokens // 32 * 16
+    halves = (pl.ds(0, middle_row), pl.ds(middle_row, tokens - middle_row))
+
+    def f_ring_copy(t, part):
+        span = halves[part]
+        return remote(f_own.at[t, span], f_ring.at[t, span], f_ring_sems, (t, part), ahead)
+
+    def reduce_task(t, part):
+        span = halves[part]
+        if part == 0:
+            f_pair_copy(t).wait_recv()
         if t == 1:
-            add(f_own.at[t], f_pair.at[t])
+            add(f_own.at[t, span], f_pair.at[t, span])
         else:
             before = t - 1 if t else last
-            f_ring_copy(before).wait_recv()
-            add(f_own.at[t], f_pair.at[t], f_ring.at[before])
+            f_ring_copy(before, part).wait_recv()
+            add(f_own.at[t, span], f_pair.at[t, span], f_ring.at[before, span])
         if t:
-            f_ring_copy(t).start()
+            f_ring_copy(t, part).start()
 
     for copy in loads[3:5]:
         copy.wait()
@@ -589,15 +599,14 @@
 
         @pl.when(j == 1)
         def _():
-            reduce_task(1)
+            reduce_task(1, 0)
+            reduce_task(1, 1)
 
     pass_cot(1, 0, True)
     pass_cot(2, 1, True)
     for t in turns[1:]:
-        reduce_task(t)
-        if t == 2:
-            pass_cot(1, 1, False)
-            pass_cot(2, 0, False)
+        for part in range(2):
+            reduce_task(t, part)
 
     stream[...] = residual[...].astype(jnp.float32) + f_own[0].astype(jnp.float32)
     y[:tokens, :] = (stream[...] * gain_ref[:, my_cols]).astype(y.dtype)
@@ -624,18 +633,21 @@
     behind_h = [lax.rem(h + hidden - 2 * t, hidden) for t in range(chips)]
     y_made = {}
 
-    def send_y(key, mine, i, t, span, device):
+    def y_copy(number, mine, i, t, span, device):
         target = x_all.at[source[i], behind_h[t], spans[span]]
-        copy = remote(
-            y.at[spans[span]] if mine else target, target, y_sems, (len(y_made),), device
-        )
-        copy.start()
-        y_made[key] = copy
+        return remote(y.at[spans[span]] if mine else target, target, y_sems, (number,), device)
+
+    def send_y(key, *what):
+        y_made[key] = (len(y_made),) + what
+        y_copy(*y_made[key]).start()
+
+    def y_arrived(*key):
+        y_copy(*y_made[key]).wait_recv()
 
     home = groups - 1
 
     def ring_y0(t):
-        y_made["ring0", t].wait_recv()
+        y_arrived("ring0", t)
         if t + 1 < chips:
             send_y(("ring0", t + 1), False, home, t, 0, ahead)
         for i in (1, 2):
@@ -643,20 +655,20 @@
         send_y(("pair", home, t, 0), False, home, t, 0, partner)
 
     def ring_y1(t, i):
-        y_made["ring1", t, i].wait_recv()
+        y_arrived("ring1", t, i)
         if t + 1 < chips:
             send_y(("ring1", t + 1, i), False, i, t, 1, ahead)
         send_y(("pair", i, t, 1), False, i, t, 1, partner)
 
     def near_y0(t):
         for i, span in ((1, "a"), (2, "b")):
-            y_made["near0", t, i].wait_recv()
+            y_arrived("near0", t, i)
             send_y(("far0", t, span), False, i, t, span, peers[3 - i])
             send_y(("pair", i, t, 0), False, i, t, 0, partner)
 
     def far_y0(t):
         for span in ("a", "b"):
-            y_made["far0", t, span].wait_recv()
+            y_arrived("far0", t, span)
             send_y(("pair", 0, t, span), False, 0, t, span, partner)
 
     local = pltpu.make_async_copy(y, x_all.at[g, h], load_sems.at[len(moves)])
@@ -669,43 +681,59 @@
     send_y(("ring1", 1, home), True, home, 0, 1, ahead)
     for span in (0, 1):
         send_y(("pair", home, 0, span), True, home, 0, span, partner)
-    pass_cot(0, 0, False)
-    pass_cot(0, 1, False)
+    pass_cot(1, 1, False)
+    pass_cot(2, 0, False)
     ring_y0(1)
     near_y0(0)
     for i in (1, 2, 0):
-        y_made["near1", i].wait_recv()
+        y_arrived("near1", i)
         send_y(("ring1", 1, i), False, i, 0, 1, ahead)
         send_y(("pair", i, 0, 1), False, i, 0, 1, partner)
     ring_y1(1, home)
+    pass_cot(0, 0, False)
+    pass_cot(0, 1, False)
     for t in range(2, chips):
         ring_y0(t)
         near_y0(t - 1)
-        far_y0(t - 2)
         for i in range(final):
             ring_y1(t - 1, i)
         ring_y1(t, home)
-    near_y0(last)
-    far_y0(last - 1)
-    for i in range(final):
-        ring_y1(last, i)
-    far_y0(last)
-    local.wait()
-    for made in (cot_made, y_made):
-        for key, copy in made.items():
-            if key[0] == "pair":
-                copy.wait_recv()
-            copy.wait_send()
-    for copy in slots:
-        copy.wait()
+        if t > 2:
+            far_y0(t - 3)
     for t in turns:
-        f_pair_copy(t).wait_send()
         if t:
-            f_ring_copy(t).wait_send()
+            f_pair_copy(t).wait_send()
+            for part in range(2):
+                f_ring_copy(t, part).wait_send()
+    f_pair_copy(0).wait_send()
     for copy in loads[5:]:
         copy.wait()
-
-    cut = first_rows(tokens)
+    local.wait()
+    for copy in slots:
+        copy.wait_recv()
+    for t in range(chips):
+        for span in (0, 1):
+            y_arrived("pair", home, t, span)
+
+    def gather_task(n):
+        if n == 0:
+            near_y0(last)
+        elif n == 1:
+            for i in range(final):
+                ring_y1(last, i)
+        elif n == 2:
+            far_y0(last - 2)
+            far_y0(last - 1)
+        else:
+            far_y0(last)
+            for key in y_made:
+                if key[0] == "pair" and key[1] != home:
+                    y_arrived(*key)
+            for key, copy in cot_made.items():
+                if key[0] == "pair":
+                    copy.wait_recv()
+
+    cut = direct_rows(tokens)
     rows = (pl.ds(0, cut), pl.ds(cut, tokens - cut))
     via = (pl.ds(0, cut // 2), pl.ds(cut // 2, cut // 2))
 
@@ -816,7 +844,10 @@
 
     def finish_ring(i):
         ring_task(i, 0)
-        peer1_copy(i).start()
+
+        @pl.when(i < final)
+        def _():
+            peer1_copy(i).start()
 
     def scale_of(slot, group):
         terms = jnp.zeros((16, width), jnp.float32)
@@ -832,18 +863,19 @@
         both = jnp.where(row == per_owner, inverse, slot_all[group])
         return jnp.concatenate([both, jnp.zeros((120, tokens), jnp.float32)], axis=0).T
 
-    start_fetch(0)
+    start_fetch(home)
 
     @pl.loop(0, groups)
-    def _(i):
+    def _(step):
+        i, one, two = (lax.rem(step + groups - 1 - d, groups) for d in range(3))
         slot = lax.rem(i, 2)
         group = pair_groups(g, i)
 
-        @pl.when(i > 0)
-        def _():
-            pair_task(i - 1, 1)
-
-        @pl.when(i < final)
+        @pl.when(step > 0)
+        def _():
+            pair_task(one, 1)
+
+        @pl.when((step > 0) & (step < final))
         def _():
             start_fetch(i + 1)
 
@@ -861,25 +893,37 @@
             weight = jnp.where(lane >= s * units, scale[:, s : s + 1], weight)
         pre_gate = dot(xs[slot], w_in[:half, :], turned) * inverse
 
-        @pl.when(i > 0)
-        def _():
-            pair_task(i - 1, 2)
+        @pl.when(step == 0)
+        def _():
+            gather_task(0)
+
+        @pl.when(step > 0)
+        def _():
+            pair_task(one, 2)
 
         pre_up = dot(xs[slot], w_in[half:, :], turned) * inverse
 
-        @pl.when(i > 0)
-        def _():
-            pair_task(i - 1, 3)
-
-        @pl.when(i > 1)
-        def _():
-            ring_task(i - 2, 3)
+        @pl.when(step == 0)
+        def _():
+            gather_task(1)
+
+        @pl.when(step > 0)
+        def _():
+            pair_task(one, 3)
+
+        @pl.when(step > 1)
+        def _():
+            ring_task(two, 3)
 
         d_act = dot(cs[slot], w_out[...], turned) * weight
 
-        @pl.when(i > 0)
-        def _():
-            pair_task(i - 1, 0)
+        @pl.when(step == 0)
+        def _():
+            gather_task(2)
+
+        @pl.when(step > 0)
+        def _():
+            pair_task(one, 0)
 
         sig = jax.nn.sigmoid(pre_gate)
         swish = pre_gate * sig
@@ -897,9 +941,9 @@
         def _(j):
             t = lax.rem(j + 1, chips)
 
-            @pl.when(i > 1)
+            @pl.when(step > 1)
             def _():
-                pair_copy(i - 2, t).wait_send()
+                pair_copy(two, t).wait_send()
 
             for whose, target, at in ((partner_h, stage, slot), (h, own, i)):
                 first = pl.multiple_of(lax.rem(whose + hidden - 2 * t, hidden) * width, width)
@@ -909,43 +953,49 @@
                 if whose is partner_h:
                     pair_copy(i, t).start()
 
-        @pl.when(i > 0)
-        def _():
-            ring_task(i - 1, 2)
-
-        @pl.when(i > 1)
-        def _():
-            finish_ring(i - 2)
+        @pl.when(step > 0)
+        def _():
+            ring_task(one, 2)
+
+        @pl.when(step > 1)
+        def _():
+            finish_ring(two)
+
+        @pl.when(step == 0)
+        def _():
+            gather_task(3)
+            start_fetch(0)
 
     for buffer in (w_gate, w_up, w_down):
         buffer[...] = jnp.zeros_like(buffer)
 
     tasks = (
-        (0, lambda: pair_task(final, 1)),
-        (1, lambda: pair_task(final, 2)),
-        (3, lambda: pair_task(final, 3)),
-        (4, lambda: ring_task(final - 1, 3)),
-        (5, lambda: pair_task(final, 0)),
-        (6, lambda: finish_task(1)),
-        (9, lambda: ring_task(final, 2)),
-        (12, lambda: finish_ring(final - 1)),
-        (15, lambda: finish_task(2)),
-        (18, lambda: ring_task(final, 3)),
-        (25, lambda: finish_task(3)),
-        (27, lambda: ring_task(final, 0)),
+        (0, lambda: pair_task(final - 1, 1)),
+        (1, lambda: pair_task(final - 1, 2)),
+        (2, lambda: pair_task(final - 1, 3)),
+        (3, lambda: pair_task(final - 1, 0)),
+        (5, lambda: ring_task(final - 2, 3)),
+        (8, lambda: ring_task(final - 1, 2)),
+        (9, lambda: finish_task(1)),
+        (11, lambda: finish_ring(final - 2)),
+        (14, lambda: ring_task(final - 1, 3)),
+        (18, lambda: finish_task(2)),
+        (22, lambda: finish_ring(final - 1)),
+        (27, lambda: finish_task(3)),
     )
 
     @pl.loop(0, groups * hidden)
     def _(n):
-        i, b = final - n // hidden, lax.rem(n, hidden)
+        turn, b = n // hidden, lax.rem(n, hidden)
+        i = lax.rem(2 * groups - 2 - turn, groups)
         slot = lax.rem(i, 2)
         group = pair_groups(g, i)
 
-        @pl.when((b == 0) & (n > 0) & (i > 0))
-        def _():
-            start_fetch(i - 1)
-
-        @pl.when((b == 0) & (i < final - 1))
+        @pl.when((b == 0) & (turn > 0) & (turn < final))
+        def _():
+            start_fetch(lax.rem(i + groups - 1, groups))
+
+        @pl.when((b == 0) & (turn > 1))
         def _():
             wait_fetch(i)
 
@@ -976,7 +1026,7 @@
     normed_out[...] = own[final, 0, 1]
     for t in range(chips):
         for i in range(groups):
-            if i + 2 >= groups:
+            if final - 2 <= i < final:
                 pair_copy(i, t).wait_send()
             if t:
                 ring1_copy(i, t).wait_send()
@@ -988,6 +1038,12 @@
             ring0_copy(t).wait_send()
     for i in range(final):
         peer1_copy(i).wait_send()
+    for key in y_made:
+        y_copy(*y_made[key]).wait_send()
+    for copy in cot_made.values():
+        copy.wait_send()
+    for copy in slots:
+        copy.wait_send()
 
 
 def store_kernel(count, *refs):
@@ -1025,7 +1081,7 @@
     per_owner = fetch_list.shape[1] // groups
     half = per_owner * units
     bf = queries.dtype
-    cut = first_rows(tokens)
+    cut = direct_rows(tokens)
     block = (2, tokens, width)
     vmem = pl.BlockSpec(memory_space=pltpu.VMEM)
     anywhere = pl.BlockSpec(memory_space=pl.ANY)
@@ -1052,7 +1108,7 @@
         ((chips, 2, cut, width), bf), ((groups, chips, 2, tokens - cut, width), bf),
     ]
     sems = [
-        (9,), (2, groups - 1), (2, 12), (2, chips), (2, chips), (2, 72), (2, 2 * hidden + 1),
+        (9,), (2, groups - 1), (2, 12), (2, chips), (2, chips, 2), (2, 72), (2, 2 * hidden + 1),
         (2, groups, chips), (2, groups, chips), (2, 2, chips), (2, groups - 2, chips),
         (2, groups - 1), (2, chips),
     ]

time: 143 us -> 140 us (0.979)
  Pallas kernels: 142 us -> 139 us
    pallas_call x1, Pallas kernels: 138 us -> 135 us  [layer(): pl.pallas_call(functools.partial(layer_kernel, groups, hidden), in_specs=...]
where the time goes in v7:
time: 140 us
  Pallas kernels  139 us (99%)
    pallas_call x1, Pallas kernels, layer(): pl.pallas_call(functools.partial(layer_kernel, groups, hidden), in_specs=...  135 us
    pallas_call x1, Pallas kernels, store(): pl.pallas_call(functools.partial(store_kernel, count), in_specs=[pl.Block...  3.91 us

profile of v7, /device:TPU:0, one launch (start us, length us, event | category | flops | bytes accessed | tf_op | source)
XLA Modules:
  0.0 139.9 jit_solution(1951272592746256402)
XLA Ops:
  0.6 135.3 %layer.1 = (bf16[384,256]{1,0:T(8,128)(2,1)S(1)}, bf16[384,256]{1,0:T(8,128)(2,1)S(1)}, bf16[8,96,2048]{2,1,0:T(8,128)(2,1)S(1)}, bf16[8,96,2048]{2,1,0:T(8,128)...) custom-call(s32[4,16]{1,0:T(4,128)} %fetch_ref.1, ...), custom_call_target="tpu_custom_call" | custom-call | tf_op jit(solution)/shard_map/layer/pallas_call | solution.py:1115
  136.0 3.9 %store.1 = (bf16[384,256]{1,0:T(8,128)(2,1)}, bf16[384,256]{1,0:T(8,128)(2,1)}, bf16[8,96,2048]{2,1,0:T(8,128)(2,1)}, bf16[8,96,2048]{2,1,0:T(8,128)(2,1)}, bf16[8,96,2048]{2,1,0:T(8,128)(2,1)}) custom-call(bf16[384,256]{1,0:T(8,128)(2,1)S(1)} %get-tuple-element.15.refs_0_, bf16[384,256]{1,0:T(8,128)(2,1)S(1)} %get-tuple-element.16.refs_1_, ...), custom_call_target="tpu_custom_call" | custom-call | tf_op jit(solution)/shard_map/store/pallas_call | solution.py:1062

commit v8 on v7

--- a/solution.py
+++ b/solution.py
@@ -442,7 +442,7 @@
 
 
 def direct_rows(count):
-    return count * 5 // 192 * 32
+    return count // 48 * 32
 
 
 def layer_kernel(

time: 140 us -> 139 us (level)
  no operation moved by 1% of the time
where the time goes in v8:
time: 139 us
  Pallas kernels  138 us (99%)
    pallas_call x1, Pallas kernels, layer(): pl.pallas_call(functools.partial(layer_kernel, groups, hidden), in_specs=...  134 us
    pallas_call x1, Pallas kernels, store(): pl.pallas_call(functools.partial(store_kernel, count), in_specs=[pl.Block...  3.91 us

profile of v8, /device:TPU:0, one launch (start us, length us, event | category | flops | bytes accessed | tf_op | source)
XLA Modules:
  0.0 138.6 jit_solution(10613807587066403544)
XLA Ops:
  0.6 134.0 %layer.1 = (bf16[384,256]{1,0:T(8,128)(2,1)S(1)}, bf16[384,256]{1,0:T(8,128)(2,1)S(1)}, bf16[8,96,2048]{2,1,0:T(8,128)(2,1)S(1)}, bf16[8,96,2048]{2,1,0:T(8,128)...) custom-call(s32[4,16]{1,0:T(4,128)} %fetch_ref.1, ...), custom_call_target="tpu_custom_call" | custom-call | tf_op jit(solution)/shard_map/layer/pallas_call | solution.py:1115
  134.7 3.9 %store.1 = (bf16[384,256]{1,0:T(8,128)(2,1)}, bf16[384,256]{1,0:T(8,128)(2,1)}, bf16[8,96,2048]{2,1,0:T(8,128)(2,1)}, bf16[8,96,2048]{2,1,0:T(8,128)(2,1)}, bf16[8,96,2048]{2,1,0:T(8,128)(2,1)}) custom-call(bf16[384,256]{1,0:T(8,128)(2,1)S(1)} %get-tuple-element.15.refs_0_, bf16[384,256]{1,0:T(8,128)(2,1)S(1)} %get-tuple-element.16.refs_1_, ...), custom_call_target="tpu_custom_call" | custom-call | tf_op jit(solution)/shard_map/store/pallas_call | solution.py:1062
